TPU v7x, 32 devices: a whole 2x2x4 slice. The times are simulated.
32 devices in a mesh: dp: 4 (over y, x), tensor: 8 (over z, core).
Axes of the slice: x: 2, y: 2, z: 4, core: 2. Of those that a mesh axis runs over, the one named last changes fastest.
Arguments:
- tokens: bfloat16 [8192, 2048], P(('dp', 'tensor')), may hold values from -6 to 6
- cotangent: bfloat16 [8192, 2048], P(('dp', 'tensor')), may hold values from -6 to 6
- first_norm_gain: float32 [2048], replicated, may hold values from 0.5 to 1.5
- w_qkv: bfloat16 [2048, 3, 2048], P(None, None, 'tensor'), may hold values from -0.125 to 0.125
- w_out: bfloat16 [2048, 2048], P('tensor'), may hold values from -0.75 to 0.75
- g_ln: float32 [2048], replicated, may hold values from 0.5 to 1.5
- b_ln: float32 [2048], replicated, may hold values from -3 to 3
- w_up: bfloat16 [2048, 8192], P(None, 'tensor'), may hold values from -0.125 to 0.125
- w_down: bfloat16 [8192, 2048], P('tensor'), may hold values from -0.0625 to 0.0625
- probs: float32 [8192], P(('dp', 'tensor')), may hold values from 0.2 to 1
- lengths: int32 [4, 8], P('dp'), may hold values from 1 to 1024, 2048 in all within a row
- head_count: int32 [4], P('dp'), may hold values from 4 to 16, as said below
- widths: int32 [8192], P('dp'), may hold values from 0 to 3, as said below
Outputs:
- out: bfloat16 [8192, 2048], P(('dp', 'tensor'))
- tokens_grad: float32 [8192, 2048], P(('dp', 'tensor'))
- probs_grad: float32 [8192], P(('dp', 'tensor'))
- g_rms_grad: float32 [2048], replicated
- w_qkv_grad: float32 [2048, 3, 2048], P('dp', None, 'tensor')
- w_out_grad: float32 [2048, 2048], P('tensor', 'dp')
- g_ln_grad: float32 [2048], replicated
- b_ln_grad: float32 [2048], replicated
- w_up_grad: float32 [2048, 8192], P('dp', 'tensor')
- w_down_grad: float32 [8192, 2048], P('tensor', 'dp')
Inputs may be any that keep to these rules, and one draw needn't show every extreme that they name: `head_count`: each packed sequence's number of active heads is a multiple of 4. `widths`: in every packed sequence each width index is held by exactly 512 tokens.
All inputs are finite; a program needn't handle non-finite values.
Results may differ from a plain program's by a relative error of at most 0.025.
Values may be sent and summed in bfloat16 or wider, within the bound.
A program may use at most 192 MiB of HBM per device.

v0:
```python
import functools

import jax
import jax.numpy as jnp
from jax import lax
from jax.experimental import pallas as pl
from jax.experimental.pallas import tpu as pltpu
from jax.sharding import PartitionSpec as P

HDIM = 128
FF = 8192
EPSILON = 1e-05
NEGATIVE = -1e30
MAXDOC = 1024
GROUPS = 8
QROWS = 256
MESH = pl.DeviceIdType.MESH
BF = jnp.bfloat16
F32 = jnp.float32
ANY = pl.BlockSpec(memory_space=pl.ANY)
VM = pl.BlockSpec(memory_space=pltpu.VMEM)
DMA = pltpu.SemaphoreType.DMA
NT = (((1,), (1,)), ((), ()))
TN = (((0,), (0,)), ((), ()))


def dot(a, b, dims=(((1,), (0,)), ((), ()))):
    return lax.dot_general(a, b, dims, preferred_element_type=F32)


class Line:
    def __init__(self, ranks, rows):
        self.ranks, self.chips, self.rows = ranks, ranks // 2, rows
        self.t = lax.axis_index("tensor")
        self.z, self.c = self.t // 2, lax.rem(self.t, 2)
        self.has_up, self.has_down = self.z < self.chips - 1, self.z > 0
        self.up = jnp.minimum(self.t + 2, ranks - 1)
        self.down = jnp.maximum(self.t - 2, 0)
        self.partner = self.t + 1 - 2 * self.c

    def barrier(self, dp_size=0):
        sem = pltpu.get_barrier_semaphore()
        pl.semaphore_signal(sem, inc=1, device_id={"tensor": self.partner}, device_id_type=MESH)

        @pl.when(self.has_up)
        def _():
            pl.semaphore_signal(sem, inc=1, device_id={"tensor": self.up}, device_id_type=MESH)

        @pl.when(self.has_down)
        def _():
            pl.semaphore_signal(sem, inc=1, device_id={"tensor": self.down}, device_id_type=MESH)

        d = lax.axis_index("dp")
        for step in range(1, dp_size):
            pl.semaphore_signal(
                sem, inc=1, device_id={"dp": lax.rem(d + step, dp_size)}, device_id_type=MESH
            )
        links = self.has_up.astype(jnp.int32) + self.has_down.astype(jnp.int32)
        pl.semaphore_wait(sem, 1 + max(dp_size - 1, 0) + links)

    def barrier_all(self, dp_size):
        sem = pltpu.get_barrier_semaphore()
        for n in range(1, self.ranks):
            pl.semaphore_signal(
                sem, inc=1, device_id={"tensor": lax.rem(self.t + n, self.ranks)}, device_id_type=MESH
            )
        d = lax.axis_index("dp")
        for n in range(1, dp_size):
            pl.semaphore_signal(
                sem, inc=1, device_id={"dp": lax.rem(d + n, dp_size)}, device_id_type=MESH
            )
        pl.semaphore_wait(sem, self.ranks - 1 + dp_size - 1)


def copy_to(src, dst, send, recv, rank):
    return pltpu.make_async_remote_copy(
        src_ref=src,
        dst_ref=dst,
        send_sem=send,
        recv_sem=recv,
        device_id={"tensor": rank},
        device_id_type=MESH,
    )


class Gather:
    def __init__(self, line, full, send, recv, across_recv):
        self.l, self.full, self.send, self.recv, self.across_recv = line, full, send, recv, across_recv

    @staticmethod
    def scratch(ranks, groups):
        return [DMA((3, ranks // 2)), DMA((groups, ranks // 2)), DMA((groups,))]

    def along(self, g, z, up):
        l = self.l
        place = self.full.at[g, z, l.c]
        return copy_to(
            place,
            place,
            self.send.at[0 if up else 1, z],
            self.recv.at[0 if g == slice(None) else g, z],
            l.up if up else l.down,
        )

    def across(self, g, column):
        place = self.full.at[g, :, column]
        return copy_to(
            place, place, self.send.at[2, 0], self.across_recv.at[0 if g == slice(None) else g], self.l.partner
        )

    def pass_on(self, g, z, up):
        @pl.when(self.l.has_up if up else self.l.has_down)
        def _():
            self.along(g, z, up).start()

    def begin(self, g):
        self.pass_on(g, self.l.z, True)
        self.pass_on(g, self.l.z, False)

    def hop(self, g, h):
        l = self.l

        @pl.when(l.z - h >= 0)
        def _():
            self.along(g, l.z - h, True).wait_recv()
            self.pass_on(g, l.z - h, True)

        @pl.when(l.z + h <= l.chips - 1)
        def _():
            self.along(g, l.z + h, False).wait_recv()
            self.pass_on(g, l.z + h, False)

        if h == l.chips - 1:
            self.across(g, l.c).start()

    def arrived(self, g):
        self.across(g, 1 - self.l.c).wait_recv()

    def drain(self):
        l, every = self.l, slice(None)
        for z in range(l.chips):

            @pl.when(l.has_up & (l.z >= z))
            def _():
                self.along(every, z, True).wait_send()

            @pl.when(l.has_down & (l.z <= z))
            def _():
                self.along(every, z, False).wait_send()

        self.across(every, l.c).wait_send()


class Reduce:
    def __init__(self, line, part, near, far, acc, send, near_recv, far_recv):
        self.l, self.part, self.near, self.far, self.acc = line, part, near, far, acc
        self.send, self.near_recv, self.far_recv = send, near_recv, far_recv

    @staticmethod
    def scratch(ranks, groups, rows, width):
        chips = ranks // 2
        return [
            pltpu.VMEM((groups, chips, 2, rows, width), BF),
            pltpu.VMEM((groups, chips, rows, width), BF),
            pltpu.VMEM((groups, chips + 1, rows, width), BF),
            pltpu.VMEM((rows, width), F32),
            DMA((groups, chips + 1)),
            DMA((groups,)),
            DMA((groups, chips + 1)),
        ]

    def across(self, g):
        l = self.l
        return copy_to(
            self.part.at[g, :, 1 - l.c],
            self.near.at[g],
            self.send.at[g, l.chips],
            self.near_recv.at[g],
            l.partner,
        )

    def along(self, g, z, up, receive=False):
        l = self.l
        at = l.z if receive else jnp.where(up, l.z + 1, l.z - 1)
        slot = z if up else jnp.where(z == at, l.chips, z)
        return copy_to(
            self.part.at[g, z, l.c],
            self.far.at[g, slot],
            self.send.at[g, z],
            self.far_recv.at[g, slot],
            l.up if up else l.down,
        ), slot

    def begin(self, g):
        self.across(g).start()

    def add(self, g, z, slots, total=None):
        side = 512

        @pl.loop(0, self.part.shape[-1] // side)
        def _(n):
            at = pl.ds(pl.multiple_of(n * side, side), side)
            value = self.part[g, z, self.l.c, :, at].astype(F32) + self.near[g, z, :, at].astype(F32)
            for slot in slots:
                value += self.far[g, slot, :, at].astype(F32)
            if total is None:
                self.part[g, z, self.l.c, :, at] = value.astype(BF)
            else:
                total[:, at] = value

    def step(self, g, d):
        l = self.l
        if d == l.chips - 1:
            self.across(g).wait_recv()

        def send(z, up):
            further = l.has_down if up else l.has_up

            @pl.when(further)
            def _():
                copy, slot = self.along(g, z, up, receive=True)
                copy.wait_recv()
                self.add(g, z, [slot])

            @pl.when(jnp.logical_not(further))
            def _():
                self.add(g, z, [])

            self.along(g, z, up)[0].start()

        @pl.when(l.z + d <= l.chips - 1)
        def _():
            send(l.z + d, True)

        @pl.when(l.z - d >= 0)
        def _():
            send(l.z - d, False)

    def last(self, g):
        l = self.l

        @pl.when(l.has_down & l.has_up)
        def _():
            self.along(g, l.z, True, receive=True)[0].wait_recv()
            self.along(g, l.z, False, receive=True)[0].wait_recv()
            self.add(g, l.z, [l.z, l.chips], self.acc)

        @pl.when(jnp.logical_not(l.has_up))
        def _():
            self.along(g, l.z, True, receive=True)[0].wait_recv()
            self.add(g, l.z, [l.z], self.acc)

        @pl.when(jnp.logical_not(l.has_down))
        def _():
            self.along(g, l.z, False, receive=True)[0].wait_recv()
            self.add(g, l.z, [l.chips], self.acc)

    def drain(self, g):
        l = self.l
        self.across(g).wait_send()
        for z in range(l.chips):

            @pl.when(l.z != z)
            def _():
                copy_to(
                    self.part.at[g, z, l.c],
                    self.far.at[g, z],
                    self.send.at[g, z],
                    self.far_recv.at[g, z],
                    l.partner,
                ).wait_send()


def within(value, limit, body):
    pl.when((value >= 0) & (value < limit))(lambda: body(value))


def swap_halves(field):
    return pltpu.roll(field, HDIM // 2, axis=1)


def call(body, ins, outs, scratch, ident, in_specs=None, out_specs=None, limit=60, flops=0, moved=0, aliases=None):
    return pl.pallas_call(
        body,
        out_shape=outs,
        in_specs=in_specs or [VM] * len(ins),
        out_specs=out_specs or [VM] * len(outs),
        scratch_shapes=scratch,
        compiler_params=pltpu.CompilerParams(
            collective_id=ident, has_side_effects=True, vmem_limit_bytes=limit << 20
        ),
        input_output_aliases=aliases or {},
        cost_estimate=pl.CostEstimate(flops=flops, bytes_accessed=moved, transcendentals=0),
    )(*ins)


def stream(line, groups, gather=None, arrived=None, reduce=None, produce=(), finish=None, lead=0, extra=None):
    hops = line.chips - 1
    produce = list(produce)
    between = len(produce) > 1
    turns = groups + hops + 1 + (lead + 1 if reduce else 0)

    @pl.loop(0, turns)
    def _(i):
        for n in range(hops):
            if gather:
                within(i - hops + n, groups, functools.partial(gather.hop, h=hops - n))
            if reduce:
                d = n + 1
                within(i - lead - 1 - hops + d, groups, functools.partial(reduce.step, d=d))
            if n == hops - 1 and gather:
                within(i, groups, gather.begin)
            if between:
                if n == 0:
                    within(i - hops - 1, groups, arrived)
                for piece in produce[n * len(produce) // hops : (n + 1) * len(produce) // hops]:
                    within(i - lead, groups, piece)
        if not between:
            for piece in produce:
                within(i - lead, groups, piece)
        if reduce:
            within(i - lead, groups, reduce.begin)
        if arrived and not between:
            within(i - hops - 1, groups, arrived)
        if reduce:

            def end(g):
                reduce.last(g)
                finish(g)

            within(i - lead - 2 - hops, groups, end)
        if extra:
            within(i, min(extra[0], turns), extra[1])

    if extra:

        @pl.loop(min(extra[0], turns), extra[0])
        def _(i):
            extra[1](i)

    if gather:
        gather.drain()
    if reduce:
        pl.loop(0, groups)(reduce.drain)


def starts_of(lengths, places):
    end, start = jnp.int32(0), jnp.zeros_like(places)
    for length in lengths:
        end = end + length
        start = start + jnp.where(places >= end, length, 0)
    return start


def softmax_block(q, k, start, first_query, first_key, scaling):
    raw = dot(k, q, NT)
    keys = first_key + lax.broadcasted_iota(jnp.int32, raw.shape, 0)
    queries = first_query + lax.broadcasted_iota(jnp.int32, raw.shape, 1)
    raw = jnp.where((keys <= queries) & (keys >= start), raw * scaling, NEGATIVE)
    exponent = jnp.exp(raw - jnp.max(raw, axis=0, keepdims=True))
    return exponent * (1.0 / jnp.sum(exponent, axis=0, keepdims=True))


def query_starts(lengths, first):
    places = first + lax.broadcasted_iota(jnp.int32, (8, QROWS), 1)
    return starts_of([lengths[0, n] for n in range(lengths.shape[1])], places)[:1]


def put_grouped(out, block, i, own_tokens, rows, at=slice(None)):
    for n in range(0, QROWS, rows):
        rank, inside = divmod(n, own_tokens)
        rank += i * (QROWS // own_tokens)
        out[inside // rows, pl.ds(pl.multiple_of(rank * rows, rows), rows), at] = block[n : n + rows]


def attend_back(qkv, grad, lengths, active, cosines, sines, width, groups, own_tokens):
    length, heads = qkv.shape[0], width // HDIM
    scaling = HDIM ** (-0.5)
    reach = MAXDOC // QROWS + 1
    rows_own = own_tokens // groups

    def body(live, docs, q, k, v, g, cos, sin, g_q, g_k, g_v, k_t, sum_k, sum_v):
        h = pl.program_id(0)

        @pl.when(live[h] == 0)
        def _():
            g_q[...] = jnp.zeros_like(g_q)
            g_k[...] = jnp.zeros_like(g_k)
            g_v[...] = jnp.zeros_like(g_v)

        def rotate_back(d, rows):
            return (d * cos[rows] + swap_halves(d * sin[rows])).astype(BF)

        @pl.when(live[h] != 0)
        def _():
            k_t[...] = k[...].T
            sum_k[...] = jnp.zeros_like(sum_k)
            sum_v[...] = jnp.zeros_like(sum_v)
            def back_block(i, count):
                low = i + 1 - count
                rows = pl.ds(pl.multiple_of(i * QROWS, QROWS), QROWS)
                keys = pl.ds(pl.multiple_of(low * QROWS, QROWS), count * QROWS)
                start = query_starts(docs, i * QROWS)
                weights = softmax_block(q[rows], k[keys], start, i * QROWS, low * QROWS, scaling)
                sum_v[keys] += dot(weights.astype(BF), g[rows])
                g_weights = dot(v[keys], g[rows], NT)
                inner = jnp.sum(weights * g_weights, axis=0, keepdims=True)
                g_scores = (weights * (g_weights - inner)).astype(BF)
                sum_k[keys] += dot(g_scores, q[rows])
                back = rotate_back(dot(k_t[:, keys], g_scores).T * scaling, rows)
                put_grouped(g_q, back, i, own_tokens, rows_own)

            for i in range(length // QROWS):
                back_block(i, min(i + 1, reach))

            for i in range(length // QROWS):
                rows = pl.ds(pl.multiple_of(i * QROWS, QROWS), QROWS)
                put_grouped(g_k, rotate_back(sum_k[rows] * scaling, rows), i, own_tokens, rows_own)
                put_grouped(g_v, sum_v[rows].astype(BF), i, own_tokens, rows_own)

    column = lambda n: pl.BlockSpec((length, HDIM), lambda h, live, docs: (0, n * heads + h))
    table = pl.BlockSpec((length, HDIM), lambda h, live, docs: (0, 0))
    return pl.pallas_call(
        body,
        out_shape=[jax.ShapeDtypeStruct((groups, length // groups, width), BF)] * 3,
        grid_spec=pltpu.PrefetchScalarGridSpec(
            num_scalar_prefetch=2,
            grid=(heads,),
            in_specs=[column(0), column(1), column(2), column(0), table, table],
            out_specs=[
                pl.BlockSpec((groups, length // groups, HDIM), lambda h, live, docs: (0, 0, h))
            ]
            * 3,
            scratch_shapes=[
                pltpu.VMEM((HDIM, length), BF),
                pltpu.VMEM((length, HDIM), F32),
                pltpu.VMEM((length, HDIM), F32),
            ],
        ),
        compiler_params=pltpu.CompilerParams(vmem_limit_bytes=48 << 20),
        cost_estimate=pl.CostEstimate(flops=10 << 30, bytes_accessed=8 << 20, transcendentals=0),
    )(active, lengths, qkv, qkv, qkv, grad, cosines, sines)


class Spread:
    def __init__(self, size, out, land, send, recv, rows=None):
        self.size, self.out, self.land, self.send, self.recv = size, out, land, send, recv
        self.rows = rows
        self.me = lax.axis_index("dp")

    def target(self, n):
        return lax.rem(self.me + n, self.size)

    def copy(self, n, source=None):
        return pltpu.make_async_remote_copy(
            src_ref=self.out.at[n],
            dst_ref=self.place(self.me if source is None else source),
            send_sem=self.send.at[n],
            recv_sem=self.recv.at[n],
            device_id={"dp": self.target(n)},
            device_id_type=MESH,
        )

    def place(self, source):
        return self.land.at[source] if self.rows is None else self.land.at[source, self.rows]

    def own(self):
        return pltpu.make_async_copy(self.out.at[0], self.place(self.me), self.send.at[0])

    def begin(self, n):
        @pl.when(n == 0)
        def _():
            self.own().start()

        @pl.when(n != 0)
        def _():
            self.copy(n).start()

    def end(self):
        self.own().wait()

        @pl.loop(1, self.size)
        def _(n):
            self.copy(n).wait_send()
            self.copy(n, lax.rem(self.me + self.size - n, self.size)).wait_recv()

    @staticmethod
    def scratch(size, shape):
        return [pltpu.VMEM((size, *shape), BF), DMA((size,)), DMA((size,))]


class Loads:
    def __init__(self, pairs, sems):
        self.copies = [
            pltpu.make_async_copy(source, held, sems.at[n]) for n, (source, held) in enumerate(pairs)
        ]

    def begin(self, first, *which):
        @pl.when(first)
        def _():
            for n in which:
                self.copies[n].start()

    def need(self, first, *which):
        @pl.when(first)
        def _():
            for n in which:
                self.copies[n].wait()


class Store:
    def __init__(self, held, out, sems, at=lambda ref, g: ref.at[g]):
        self.held, self.out, self.sems, self.at = held, out, sems, at

    def copy(self, g):
        return pltpu.make_async_copy(self.at(self.held, g), self.at(self.out, g), self.sems.at[g])

    def put(self, g):
        self.copy(g).start()

    def end(self, g):
        self.copy(g).wait()


class Turns:
    def __init__(self, pairs, sems, at=lambda ref, g: ref.at[g]):
        self.pairs, self.sems, self.at = pairs, sems, at

    def each(self, g):
        return [
            pltpu.make_async_copy(held.at[lax.rem(g, 2)], self.at(out, g), self.sems.at[n, g])
            for n, (held, out) in enumerate(self.pairs)
        ]

    def free(self, g):
        @pl.when(g >= 2)
        def _():
            for copy in self.each(g - 2):
                copy.wait()

        return lax.rem(g, 2)

    def put(self, g):
        for copy in self.each(g):
            copy.start()

    def end(self, groups):
        for g in range(max(groups - 2, 0), groups):
            for copy in self.each(g):
                copy.wait()


def scratch_of(*arrays):
    return [pltpu.VMEM(a.shape, a.dtype) for a in arrays]


def row_mean(field):
    return jnp.mean(field, axis=1, keepdims=True)


def layer_norm(resid):
    centred = resid - row_mean(resid)
    inv_std = lax.rsqrt(row_mean(centred * centred) + EPSILON)
    return centred * inv_std, inv_std


def front(
    tokens, cotangent, probs, gain, lengths, frequency, live, w_qkv, w_out, g_ln, b_ln, w_up, w_down, widths, ranks
):
    width, columns = w_out.shape[0], w_up.shape[1]
    tile = min(256, columns)
    groups, rows, model = tokens.shape
    heads = width // HDIM
    chips = ranks // 2
    own_tokens = groups * rows
    length = ranks * own_tokens
    shift = rows.bit_length() - 1
    scaling = HDIM ** (-0.5)
    reach = MAXDOC // QROWS + 1
    span = QROWS // own_tokens
    blocks = length // QROWS
    lead = 2
    hops = chips - 1
    tokens_all = ranks * rows
    normed_at = lead + 2 + hops
    hidden_at = normed_at + hops + 1
    back_at = hidden_at + 2 + hops

    def body(
        x_ref, dy, p, gain_ref, docs, freq, live_ref, w, wo, gain2, bias2, up, down, wide,
        qkv, kept_x, cos_out, sin_out, attended, resid, kept_grad, grad_resid, grad_low, gains, kept_ln, squared,
        hidden_grad,
        full, w_v, wo_v, dy_v, up_v, down_v, qkv_v, cos_v, sin_v, v_t, attended_v, low_v, resid_v, high_v, grad_v,
        lifted, squared_v, hidden_v,
        a_send, a_recv, a_across, b_send, b_recv, b_across, c_send, c_recv, c_across,
        part, near, far, acc, s1, s2, s3, t1, t2, t3,
        load_sem, kept_sem, out_sem, place_sem, attended_sem, resid_sem, result_sem, tile_sem,
    ):
        line = Line(ranks, rows)
        loads = Loads([(w, w_v), (wo, wo_v), (dy, dy_v), (up, up_v), (down, down_v)], load_sem)

        @pl.loop(0, groups)
        def _(g):
            x = x_ref[g].astype(F32)
            normal = x * lax.rsqrt(row_mean(x * x) + EPSILON) * gain_ref[...]
            full[g, line.z, line.c] = normal.astype(BF)

        line.barrier()
        gather = Gather(line, full, a_send, a_recv, a_across)
        tables = Turns([(cos_v, cos_out), (sin_v, sin_out)], out_sem.at[pl.ds(1, 2)], lambda ref, g: ref.at[:, g])
        stores = [
            Store(full, kept_x, kept_sem.at[0]),
            Store(qkv_v, qkv, out_sem.at[0], lambda ref, g: ref.at[:, g]),
        ]
        place_grad = pltpu.make_async_copy(low_v, kept_grad.at[:, line.z, line.c], place_sem)

        def scale_grad(turn):
            loads.begin(turn == 0, 0, 1, 2)

            @pl.when(turn == 1)
            def _():
                loads.need(True, 2)

                @pl.loop(0, groups)
                def _(g):
                    low_v[g] = (dy_v[g].astype(F32) * p[g, :, :1]).astype(BF)

                place_grad.start()

        def project(g):
            r = lax.broadcasted_iota(jnp.int32, (ranks * rows, HDIM), 0)
            lane = lax.broadcasted_iota(jnp.int32, (ranks * rows, HDIM), 1)
            places = lax.shift_right_logical(r, shift) * own_tokens + g * rows + (r & (rows - 1))
            starts = starts_of([docs[0, n] for n in range(docs.shape[1])], places)
            angles = (places - starts).astype(F32) * freq[...]
            c = jnp.cos(angles)
            s = jnp.sin(angles)
            s = jnp.where(lane < HDIM // 2, -s, s)
            slot = tables.free(g)
            for rank in range(ranks):
                cos_v[slot, rank] = c[rank * rows : (rank + 1) * rows]
                sin_v[slot, rank] = s[rank * rows : (rank + 1) * rows]
            tables.put(g)
            gather.arrived(g)
            loads.need(g == 0, 0)
            x = full[g].reshape(ranks * rows, model)
            for which in range(3):
                out = dot(x, w_v[which])
                for h in range(heads):
                    u = out[:, h * HDIM : (h + 1) * HDIM]
                    if which < 2:
                        u = u * c + swap_halves(u) * s
                    u = u.astype(BF)
                    at = (which * heads + h) * HDIM
                    for rank in range(ranks):
                        qkv_v[rank, g, :, at : at + HDIM] = u[rank * rows : (rank + 1) * rows]
            for store in stores:
                store.put(g)

        stream(line, groups, gather, arrived=project, extra=(2, scale_grad))

        @pl.loop(0, groups)
        def _(g):
            for store in stores:
                store.end(g)

        tables.end(groups)
        loads.begin(True, 3, 4)
        second = Gather(line, kept_grad, b_send, b_recv, b_across)
        third = Gather(line, full, c_send, c_recv, c_across)
        reduce = Reduce(line, part, near, far, acc, s1, s2, s3)
        reduce_back = Reduce(line, part, near, far, acc, t1, t2, t3)
        keep = Store(attended_v, attended, attended_sem)
        keep_ln = Store(full, kept_ln, kept_sem.at[1])
        keep_resid = Store(resid_v, resid, resid_sem)
        keep_low = Store(low_v, grad_low, result_sem)
        highs = Turns([(high_v, grad_resid)], tile_sem.at[pl.ds(1, 1)])
        hiddens = Turns([(squared_v, squared), (hidden_v, hidden_grad)], tile_sem.at[pl.ds(2, 2)])
        gains[...] = jnp.zeros_like(gains)
        first_column = line.t * columns
        place_grad.wait()

        def fetch(g):
            slot = lax.rem(g, 2)
            return pltpu.make_async_copy(kept_grad.at[g], grad_v.at[slot], tile_sem.at[0, slot])

        def part_of(which, h):
            return pl.ds(pl.multiple_of((which * heads + h) * HDIM, HDIM), HDIM)

        def attend_block(i, count):
            low = i + 1 - count
            start = query_starts(docs, i * QROWS)

            @pl.loop(0, heads)
            def _(h):
                q = qkv_v[pl.ds(i * span, span), :, :, part_of(0, h)].reshape(QROWS, HDIM)
                k = qkv_v[pl.ds(low * span, count * span), :, :, part_of(1, h)].reshape(count * QROWS, HDIM)
                weights = softmax_block(q, k, start, i * QROWS, low * QROWS, scaling)
                keys = pl.ds(pl.multiple_of(low * QROWS, QROWS), count * QROWS)
                done = dot(v_t[h, :, keys], weights.astype(BF)).T
                done = (done * live_ref[:, part_of(0, h)]).astype(BF)
                put_grouped(attended_v, done, i, own_tokens, rows, part_of(0, h))

        def attention(turn):
            @pl.when(turn == 0)
            def _():
                @pl.loop(0, heads)
                def _(h):
                    v_t[h] = qkv_v[:, :, :, part_of(2, h)].reshape(length, HDIM).T

                for i in range(min(reach - 1, blocks)):
                    attend_block(i, i + 1)

            @pl.when(turn == 1)
            def _():
                @pl.loop(reach - 1, blocks)
                def _(i):
                    attend_block(i, reach)

        def produce(g):
            keep.put(g)
            loads.need(g == 0, 1)
            for n in range(0, model, 512):
                out = dot(attended_v[g], wo_v[:, n : n + 512]).astype(BF)
                part[g, ..., n : n + 512] = out.reshape(chips, 2, rows, 512)

        def norm(g):
            reduce.last(g)
            total = x_ref[g].astype(F32) + acc[...]
            resid_v[g] = total
            keep_resid.put(g)
            lhat, _ = layer_norm(total)
            full[g, line.z, line.c] = (lhat * gain2[...] + bias2[...]).astype(BF)
            third.begin(g)

        def arrived(g):
            third.arrived(g)
            keep_ln.put(g)
            reduce.drain(g)

            @pl.when(g == 0)
            def _():
                fetch(0).start()

            fetch(g).wait()

            @pl.when(g + 1 < groups)
            def _():
                fetch(g + 1).start()

            loads.need(g == 0, 3, 4)

        def forward(g):
            slot = hiddens.free(g)
            limit = (jnp.broadcast_to(wide[pl.ds(g, 1), :], (HDIM, tokens_all)).T[:, :1] + 1) * (FF // 4)

            @pl.loop(0, columns // tile)
            def _(n):
                at = pl.ds(pl.multiple_of(n * tile, tile), tile)
                hidden = dot(full[g].reshape(tokens_all, model), up_v[:, at])
                ids = first_column + n * tile + lax.broadcasted_iota(jnp.int32, hidden.shape, 1)
                live = jnp.where(ids < limit, jnp.maximum(hidden, 0.0), 0.0)
                lifted[:, at] = live
                squared_v[slot, :, at] = (live * live).astype(BF)

        def backward(g):
            slot = lax.rem(g, 2)

            @pl.loop(0, columns // tile)
            def _(n):
                at = pl.ds(pl.multiple_of(n * tile, tile), tile)
                back = dot(grad_v[slot].reshape(tokens_all, model), down_v[at, :], NT)
                hidden_v[slot, :, at] = (back * (2.0 * lifted[:, at])).astype(BF)

            hiddens.put(g)

        def lower(g):
            slot = lax.rem(g, 2)

            @pl.loop(0, model // 256)
            def _(n):
                at = pl.ds(pl.multiple_of(n * 256, 256), 256)
                out = dot(hidden_v[slot], up_v[at, :], NT).astype(BF)
                part[g, :, :, :, at] = out.reshape(chips, 2, rows, 256)

        def finish(g):
            reduce_back.last(g)
            lhat, inv_std = layer_norm(resid_v[g])
            back = acc[...]
            gains[0:1] += jnp.sum(back * lhat, axis=0, keepdims=True)
            gains[1:2] += jnp.sum(back, axis=0, keepdims=True)
            back = back * gain2[...]
            back = dy_v[g].astype(F32) + inv_std * (back - row_mean(back) - lhat * row_mean(back * lhat))
            high_v[highs.free(g)] = back
            low_v[g] = back.astype(BF)
            highs.put(g)
            keep_low.put(g)

        @pl.loop(0, groups + back_at)
        def _(i):
            for n in range(hops):
                h, d = hops - n, n + 1
                within(i - hidden_at - 1 - hops + d, groups, functools.partial(reduce_back.step, d=d))
                within(i - normed_at - h, groups, functools.partial(third.hop, h=h))
                within(i - lead - 1 - hops + d, groups, functools.partial(reduce.step, d=d))
                within(i - h, groups, functools.partial(second.hop, h=h))
                if n == 0:
                    within(i - hidden_at, groups, arrived)
                for piece in (forward, backward, lower)[n * 3 // hops : (n + 1) * 3 // hops]:
                    within(i - hidden_at, groups, piece)
            within(i, groups, second.begin)
            within(i - hidden_at, groups, reduce_back.begin)
            within(i - normed_at, groups, norm)
            within(i - lead, groups, produce)
            within(i - lead, groups, reduce.begin)
            within(i - hops - 1, groups, second.arrived)
            within(i - back_at, groups, finish)
            within(i, lead, attention)

        second.drain()
        third.drain()
        pl.loop(0, groups)(reduce_back.drain)

        @pl.loop(0, groups)
        def _(g):
            for store in (keep, keep_ln, keep_resid, keep_low):
                store.end(g)

        highs.end(groups)
        hiddens.end(groups)

    table = jax.ShapeDtypeStruct((ranks, groups, rows, HDIM), F32)
    projected = jax.ShapeDtypeStruct((ranks, groups, rows, 3 * width), BF)
    full = jax.ShapeDtypeStruct((groups, chips, 2, rows, model), BF)
    attended = jax.ShapeDtypeStruct((groups, tokens_all, width), BF)
    high = jax.ShapeDtypeStruct((groups, rows, model), F32)
    low = jax.ShapeDtypeStruct((groups, rows, model), BF)
    hidden = jax.ShapeDtypeStruct((groups, tokens_all, columns), BF)
    return call(
        body,
        [tokens, cotangent, probs, gain, lengths, frequency, live, w_qkv, w_out, g_ln, b_ln, w_up, w_down, widths],
        [
            projected,
            full,
            table,
            table,
            attended,
            high,
            full,
            high,
            low,
            jax.ShapeDtypeStruct((2, model), F32),
            full,
            hidden,
            hidden,
        ],
        [
            *scratch_of(full, w_qkv, w_out, cotangent, w_up, w_down, projected),
            pltpu.VMEM((2, ranks, rows, HDIM), F32),
            pltpu.VMEM((2, ranks, rows, HDIM), F32),
            pltpu.VMEM((heads, HDIM, length), BF),
            *scratch_of(attended, low, high),
            pltpu.VMEM((2, rows, model), F32),
            pltpu.VMEM((2, chips, 2, rows, model), BF),
            pltpu.VMEM((tokens_all, columns), F32),
            pltpu.VMEM((2, tokens_all, columns), BF),
            pltpu.VMEM((2, tokens_all, columns), BF),
            *Gather.scratch(ranks, groups) * 3,
            *Reduce.scratch(ranks, groups, rows, model),
            *Reduce.scratch(ranks, groups, rows, model)[-3:],
            DMA((5,)),
            DMA((2, groups)),
            DMA((3, groups)),
            DMA,
            *[DMA((groups,))] * 3,
            DMA((4, groups)),
        ],
        0,
        in_specs=[VM, ANY, VM, VM, pl.BlockSpec(memory_space=pltpu.SMEM), VM, VM, ANY, ANY, VM, VM, ANY, ANY, VM],
        out_specs=[ANY] * 9 + [VM] + [ANY] * 3,
        flops=8 * length * model * (width + columns),
        moved=160 << 20,
    )


def hidden_weights(spread, inputs, hidden, first, turn_of, columns):
    n = turn_of
    side = min(256, spread.out.shape[1])

    @pl.loop(0, spread.out.shape[1] // side)
    def _(m):
        at = pl.ds(pl.multiple_of(first + m * side, side), side)
        to = pl.ds(pl.multiple_of(m * side, side), side)
        x = inputs[:, :, at]
        spread.out[n, to] = dot(
            x.reshape(x.shape[0] * x.shape[1], side), hidden[...].reshape(-1, columns), TN
        ).astype(BF)

    spread.begin(n)


def feed_out(
    own_grad, squared, hidden_grad, kept_ln, branch_grad, w_down, w_out, active, resid, cotangent, probs, ranks, sequences
):
    groups, rows, model = own_grad.shape
    columns, width = w_down.shape[0], w_out.shape[0]
    tokens = ranks * rows
    share = model // sequences
    half = share // 2

    def body(
        own, sq, hg, ln, bg, down, w, live, res, dy, p, result, probs_grad, kept, grad, land_down, land_up,
        full, g_send, g_recv, g_across, part, near, far, acc, s1, s2, s3, kept_sem,
        out_down, down_send, down_recv, out_up, up_send, up_recv, ln_v, bg_v, fetch_sem,
        sq_v, hg_v, down_v, res_v, dy_v, load_sem, result_v, back_v, result_sem, back_sem,
    ):
        line = Line(ranks, rows)
        gather = Gather(line, full, g_send, g_recv, g_across)
        reduce = Reduce(line, part, near, far, acc, s1, s2, s3)
        to_down = Spread(sequences, out_down, land_down, down_send, down_recv)
        to_up = Spread(sequences, out_up, land_up, up_send, up_recv, pl.ds(0, half))
        keep = Store(full, kept, kept_sem)
        keep_result = Store(result_v, result, result_sem)
        keep_back = Store(back_v, grad, back_sem, lambda ref, g: ref.at[:, g])

        def arrived(g):
            gather.arrived(g)
            keep.put(g)
            back = (dot(full[g].reshape(tokens, model), w[...], NT) * live[...]).astype(BF)
            for rank in range(ranks):
                back_v[rank, g] = back[rank * rows : (rank + 1) * rows]
            keep_back.put(g)

        def produce(g):
            loads.need(g == 0, 0, 1)

            @pl.loop(0, model // 256)
            def _(n):
                at = pl.ds(pl.multiple_of(n * 256, 256), 256)
                out = dot(sq_v[g], down_v[:, at]).astype(BF)
                part[g, :, :, :, at] = out.reshape(ranks // 2, 2, rows, 256)

        def finish(g):
            loads.need(g == 0, 3, 4)
            ffn = acc[...]
            result_v[g] = (res_v[g] + p[g, :, :1] * ffn).astype(BF)
            keep_result.put(g)
            probs_grad[g] = jnp.broadcast_to(
                jnp.sum(dy_v[g].astype(F32) * ffn, axis=1, keepdims=True), (rows, HDIM)
            )

        def fetches(step):
            at = pl.multiple_of(to_up.target(lax.rem(step + 1, sequences)) * share, share)
            return [
                pltpu.make_async_copy(ln.at[:, :, pl.ds(at, half)], ln_v, fetch_sem.at[0]),
                pltpu.make_async_copy(bg.at[:, :, pl.ds(at, share)], bg_v, fetch_sem.at[1]),
            ]

        def weights(step):
            n = lax.rem(step + 1, sequences)
            loads.need(step == 0, 2)
            for fetch in fetches(step):
                fetch.wait()
            side = min(256, columns)

            @pl.loop(0, columns // side)
            def _(m):
                at = pl.ds(pl.multiple_of(m * side, side), side)
                out_down[n, at] = dot(
                    sq_v[:, :, at].reshape(groups * tokens, side), bg_v[...].reshape(groups * tokens, share), TN
                ).astype(BF)

            to_down.begin(n)
            hidden_weights(to_up, ln_v, hg_v, 0, n, columns)

            @pl.when(step + 1 < sequences)
            def _():
                for fetch in fetches(step + 1):
                    fetch.start()

        def beside(turn):
            loads.begin(turn == 0, 0, 1, 2)

            @pl.when(turn == 0)
            def _():
                for fetch in fetches(0):
                    fetch.start()

            loads.begin(turn == 3, 3, 4)
            within(turn - 1, sequences, weights)

        loads = Loads(
            [
                (sq, sq_v),
                (down, down_v),
                (hg, hg_v),
                (res, res_v),
                (dy, dy_v),
                (own, full.at[:, line.z, line.c]),
            ],
            load_sem,
        )
        loads.begin(True, 5)
        line.barrier(sequences)
        loads.need(True, 5)
        stream(
            line, groups, gather, arrived, reduce, [produce], finish, 1, (max(sequences + 1, 4), beside)
        )

        @pl.loop(0, groups)
        def _(g):
            for store in (keep, keep_result, keep_back):
                store.end(g)

        to_down.end()
        to_up.end()

    kept = jax.ShapeDtypeStruct((groups, ranks // 2, 2, rows, model), BF)
    low = jax.ShapeDtypeStruct((groups, rows, model), BF)
    back = jax.ShapeDtypeStruct((ranks, groups, rows, width), BF)
    return call(
        body,
        [own_grad, squared, hidden_grad, kept_ln, branch_grad, w_down, w_out, active, resid, cotangent, probs],
        [
            low,
            jax.ShapeDtypeStruct((groups, rows, HDIM), F32),
            kept,
            back,
            jax.ShapeDtypeStruct((sequences, columns, share), BF),
            jax.ShapeDtypeStruct((sequences, share, columns), BF),
        ],
        [
            *scratch_of(kept),
            *Gather.scratch(ranks, groups),
            *Reduce.scratch(ranks, groups, rows, model),
            DMA((groups,)),
            *Spread.scratch(sequences, (columns, share)),
            *Spread.scratch(sequences, (half, columns)),
            pltpu.VMEM((groups, tokens, half), BF),
            pltpu.VMEM((groups, tokens, share), BF),
            DMA((2,)),
            *scratch_of(squared, hidden_grad, w_down, resid, cotangent),
            DMA((6,)),
            *scratch_of(low, back),
            DMA((groups,)),
            DMA((groups,)),
        ],
        3,
        in_specs=[ANY, ANY, ANY, ANY, ANY, ANY, VM, VM, ANY, ANY, VM],
        out_specs=[ANY, VM, ANY, ANY, ANY, ANY],
        flops=2 * groups * tokens * model * (3 * columns + width),
        moved=100 << 20,
    )


def project_back(
    grads, w_qkv, kept_x, attended, attn_grad, kept_ln, hidden_grad, landed_up, tokens, gain, grad_resid, gains, ranks, sequences
):
    groups, tokens_all, width = grads[0].shape
    rows = tokens_all // ranks
    model = w_qkv.shape[1]
    columns = hidden_grad.shape[2]
    share = model // sequences
    half = share // 2

    def body(
        gq, gk, gv, w, xs, a, ga, ln, hg, up_in, x_ref, gain_ref, g_res, gain_parts,
        tokens_grad, totals, land_qkv, land_out, land_up,
        part, near, far, acc, s1, s2, s3,
        out_qkv, qkv_send, qkv_recv, out_out, out_send, out_recv, out_up, up_send, up_recv,
        x_v, ga_v, ln_v, fetch_sem, group_v, group_sem, w_v, a_v, hg_v, own_v, res_v, load_sem,
        mine, terms, t_send, t_recv, sums, d_send, d_recv, g_q, g_k, g_v, grad_v, grad_sem,
    ):
        line = Line(ranks, rows)
        me = lax.axis_index("dp")
        reduce = Reduce(line, part, near, far, acc, s1, s2, s3)
        to_qkv = Spread(sequences, out_qkv, land_qkv, qkv_send, qkv_recv)
        to_out = Spread(sequences, out_out, land_out, out_send, out_recv)
        to_up = Spread(sequences, out_up, land_up, up_send, up_recv, pl.ds(half, half))
        parts = (g_q, g_k, g_v)
        loads = Loads(
            [(w, w_v), (a, a_v), (hg, hg_v), (x_ref, own_v), (g_res, res_v), (gq, g_q), (gk, g_k), (gv, g_v)],
            load_sem,
        )
        keep_grad = Store(grad_v, tokens_grad, grad_sem)

        def group_fetch(g):
            slot = lax.rem(g, 2)
            return pltpu.make_async_copy(xs.at[g], group_v.at[slot], group_sem.at[slot])

        loads.begin(True, 0, 5, 6, 7)
        group_fetch(0).start()
        mine[0:1] = jnp.zeros((1, model), F32)
        mine[1:3] = gain_parts[...]

        def produce(g):
            loads.need(g == 0, 0, 5, 6, 7)
            group_fetch(g).wait()

            @pl.when(g + 1 < groups)
            def _():
                group_fetch(g + 1).start()

            slot = lax.rem(g, 2)

            @pl.loop(0, model // 256)
            def _(n):
                at = pl.ds(pl.multiple_of(n * 256, 256), 256)
                out = dot(g_q[g], w_v[0, at], NT)
                out += dot(g_k[g], w_v[1, at], NT)
                out += dot(g_v[g], w_v[2, at], NT)
                part[g, :, :, :, at] = out.astype(BF).reshape(ranks // 2, 2, rows, 256)
                mine[0:1, at] += jnp.sum(out * group_v[slot, :, at].astype(F32), axis=0, keepdims=True)

        def finish(g):
            loads.need(g == 0, 3, 4)
            x = own_v[g].astype(F32)
            scale = lax.rsqrt(row_mean(x * x) + EPSILON)
            hat = x * scale
            back = acc[...] * gain_ref[...]
            grad_v[g] = res_v[g] + scale * (back - hat * row_mean(back * hat))
            keep_grad.put(g)

        def fetches(step):
            at = pl.multiple_of(to_qkv.target(lax.rem(step + 1, sequences)) * share, share)
            return [
                pltpu.make_async_copy(ln.at[:, :, pl.ds(at + half, half)], ln_v, fetch_sem.at[0]),
                pltpu.make_async_copy(xs.at[:, :, pl.ds(at, share)], x_v, fetch_sem.at[1]),
                pltpu.make_async_copy(ga.at[:, :, pl.ds(at, share)], ga_v, fetch_sem.at[2]),
            ]

        def weights(piece):
            step = piece // 2
            n = lax.rem(step + 1, sequences)

            @pl.when(lax.rem(piece, 2) == 0)
            def _():
                loads.need(step == 0, 1, 2)
                fetches(step)[0].wait()
                hidden_weights(to_up, ln_v, hg_v, 0, n, columns)

                @pl.when(step + 1 < sequences)
                def _():
                    fetches(step + 1)[0].start()

            @pl.when(lax.rem(piece, 2) == 1)
            def _():
                for fetch in fetches(step)[1:]:
                    fetch.wait()

                @pl.loop(0, share // 256)
                def _(m):
                    at = pl.ds(pl.multiple_of(m * 256, 256), 256)
                    x = x_v[:, :, at].reshape(groups * tokens_all, 256)
                    for which in range(3):
                        out_qkv[n, which, at] = dot(
                            x, parts[which][...].reshape(groups * tokens_all, width), TN
                        ).astype(BF)

                to_qkv.begin(n)
                out_out[n] = dot(
                    a_v[...].reshape(groups * tokens_all, width), ga_v[...].reshape(groups * tokens_all, share), TN
                ).astype(BF)
                to_out.begin(n)

                @pl.when(step + 1 < sequences)
                def _():
                    for fetch in fetches(step + 1)[1:]:
                        fetch.start()

        def to_rank(n, source=None):
            return copy_to(
                mine,
                terms.at[line.t if source is None else source],
                t_send.at[n],
                t_recv.at[n],
                lax.rem(line.t + n, ranks),
            )

        def to_sequence(n, source=None):
            return pltpu.make_async_remote_copy(
                src_ref=sums.at[me],
                dst_ref=sums.at[me if source is None else source],
                send_sem=d_send.at[n],
                recv_sem=d_recv.at[n],
                device_id={"dp": lax.rem(me + n, sequences)},
                device_id_type=MESH,
            )

        def beside(turn):
            loads.begin(turn == 0, 1, 2)
            loads.begin(turn == 2, 3, 4)

            @pl.when(turn == 0)
            def _():
                for fetch in fetches(0):
                    fetch.start()

            within(turn - 1, 2 * sequences, weights)

            @pl.when(turn == groups)
            def _():
                mine[0:1] = mine[0:1] / gain_ref[...]
                terms[line.t] = mine[...]

                @pl.loop(1, ranks)
                def _(n):
                    to_rank(n).start()

            @pl.when(turn == groups + 1)
            def _():
                @pl.loop(1, ranks)
                def _(n):
                    to_rank(n).wait_send()
                    to_rank(n, lax.rem(line.t + ranks - n, ranks)).wait_recv()

                total = terms[0]
                for n in range(1, ranks):
                    total += terms[n]
                sums[me] = total

                @pl.loop(1, sequences)
                def _(n):
                    to_sequence(n).start()

            @pl.when(turn == groups + 2)
            def _():
                @pl.loop(1, sequences)
                def _(n):
                    to_sequence(n).wait_send()
                    to_sequence(n, lax.rem(me + sequences - n, sequences)).wait_recv()

                total = sums[0]
                for n in range(1, sequences):
                    total += sums[n]
                totals[...] = total

        line.barrier_all(sequences)
        stream(
            line, groups, None, None, reduce, [produce], finish, extra=(max(groups + 3, 2 * sequences + 1), beside)
        )

        @pl.loop(0, groups)
        def _(g):
            keep_grad.end(g)

        to_qkv.end()
        to_out.end()
        to_up.end()

    return call(
        body,
        [*grads, w_qkv, kept_x, attended, attn_grad, kept_ln, hidden_grad, landed_up, tokens, gain, grad_resid, gains],
        [
            jax.ShapeDtypeStruct((groups, rows, model), F32),
            jax.ShapeDtypeStruct((3, model), F32),
            jax.ShapeDtypeStruct((sequences, 3, share, width), BF),
            jax.ShapeDtypeStruct((sequences, width, share), BF),
            jax.ShapeDtypeStruct(landed_up.shape, BF),
        ],
        [
            *Reduce.scratch(ranks, groups, rows, model),
            *Spread.scratch(sequences, (3, share, width)),
            *Spread.scratch(sequences, (width, share)),
            *Spread.scratch(sequences, (half, columns)),
            pltpu.VMEM((groups, tokens_all, share), BF),
            pltpu.VMEM((groups, tokens_all, share), BF),
            pltpu.VMEM((groups, tokens_all, half), BF),
            DMA((3,)),
            pltpu.VMEM((2, tokens_all, model), BF),
            DMA((2,)),
            *scratch_of(w_qkv, attended, hidden_grad, tokens, grad_resid),
            DMA((8,)),
            pltpu.VMEM((3, model), F32),
            pltpu.VMEM((ranks, 3, model), F32),
            DMA((ranks,)),
            DMA((ranks,)),
            pltpu.VMEM((sequences, 3, model), F32),
            DMA((sequences,)),
            DMA((sequences,)),
            *scratch_of(*grads, grad_resid),
            DMA((groups,)),
        ],
        4,
        in_specs=[ANY] * 11 + [VM, ANY, VM],
        out_specs=[ANY, VM, ANY, ANY, ANY],
        flops=12 * groups * tokens_all * model * width,
        moved=60 << 20,
        aliases={9: 4},
    )


def shards(
    tokens,
    cotangent,
    first_norm_gain,
    w_qkv,
    w_out,
    g_ln,
    b_ln,
    w_up,
    w_down,
    probs,
    lengths,
    head_count,
    widths,
):
    length_all = widths.shape[0]
    own_tokens, model = tokens.shape
    ranks = length_all // own_tokens
    sequences = lax.axis_size("dp")
    groups, rows = GROUPS, own_tokens // GROUPS
    width = w_out.shape[0]
    heads_here = width // HDIM
    half = HDIM // 2
    frequency = 10000.0 ** (-jnp.arange(half, dtype=F32) / half)
    frequency = jnp.concatenate([frequency, frequency]).reshape(1, HDIM)
    w_qkv_t = w_qkv.transpose(1, 0, 2)
    x = tokens.reshape(groups, rows, model)
    dy = cotangent.reshape(groups, rows, model)
    first_norm_gain, g_ln, b_ln = (v.reshape(1, model) for v in (first_norm_gain, g_ln, b_ln))
    p = jnp.broadcast_to(probs.reshape(groups, rows, 1), (groups, rows, HDIM))
    head_ids = lax.axis_index("tensor") * heads_here + jnp.arange(heads_here, dtype=jnp.int32)
    active = (head_ids < head_count[0]).astype(jnp.int32)
    live = jnp.repeat(active.astype(F32), HDIM).reshape(1, width)
    wide = widths.reshape(ranks, groups, rows).swapaxes(0, 1).reshape(groups, ranks * rows)

    (
        qkv, kept_x, cosines, sines, attended, resid, kept_ffn_grad, grad_resid, grad_low, gains, kept_ln, squared,
        grad_hidden,
    ) = front(
        x, dy, p, first_norm_gain, lengths, frequency, live, w_qkv_t, w_out, g_ln, b_ln, w_up, w_down, wide, ranks
    )
    qkv = qkv.reshape(length_all, 3 * width)
    cosines, sines = cosines.reshape(length_all, HDIM), sines.reshape(length_all, HDIM)
    whole = lambda kept: kept.reshape(groups, ranks * rows, model)
    result, probs_grad, kept_attn_grad, grad_attended, land_down, land_up = feed_out(
        grad_low, squared, grad_hidden, whole(kept_ln), whole(kept_ffn_grad), w_down, w_out, live, resid, dy, p, ranks, sequences
    )
    grad_proj = attend_back(
        qkv,
        grad_attended.reshape(length_all, width),
        lengths,
        active,
        cosines,
        sines,
        width,
        groups,
        own_tokens,
    )
    tokens_grad, totals, land_qkv, land_out, land_up = project_back(
        grad_proj, w_qkv_t, whole(kept_x), attended, whole(kept_attn_grad), whole(kept_ln), grad_hidden, land_up, x, first_norm_gain,
        grad_resid, gains, ranks, sequences,
    )
    add_up = lambda landed: jnp.sum(landed.astype(F32), axis=0)
    return (
        result.reshape(own_tokens, model),
        tokens_grad.reshape(own_tokens, model),
        probs_grad[:, :, 0].reshape(own_tokens),
        totals[0],
        add_up(land_qkv).transpose(1, 0, 2),
        add_up(land_out),
        totals[1],
        totals[2],
        add_up(land_up),
        add_up(land_down),
    )


def solution(mesh):
    placed = (
        P(("dp", "tensor"), None),
        P(("dp", "tensor"), None),
        P(),
        P(None, None, "tensor"),
        P("tensor", None),
        P(),
        P(),
        P(None, "tensor"),
        P("tensor", None),
        P(("dp", "tensor")),
        P("dp", None),
        P("dp"),
        P("dp"),
    )
    return jax.shard_map(
        shards,
        mesh=mesh,
        in_specs=placed,
        out_specs=(
            P(("dp", "tensor"), None),
            P(("dp", "tensor"), None),
            P(("dp", "tensor")),
            P(),
            P("dp", None, "tensor"),
            P("tensor", "dp"),
            P(),
            P(),
            P("dp", "tensor"),
            P("tensor", "dp"),
        ),
        check_vma=False,
    )
```

profile of v0, /device:TPU:0, one launch (start us, length us, event | category | flops | bytes accessed | tf_op | source)
XLA Modules:
  0.0 540.0 jit_solution(14606704274515253981)
XLA Ops:
  1.3 0.6 broadcast_in_dim.12
  1.9 0.6 maximum_bitcast_fusion.freq
  2.5 0.8 broadcast_in_dim.10
  3.3 0.8 reshape.83
  4.1 0.7 reshape.84.wide
  4.7 0.8 broadcast_in_dim.11.p
  5.5 296.5 %shard_map.204 = (bf16[8,8,32,768]{3,2,1,0:T(8,128)(2,1)}, bf16[8,4,2,32,2048]{4,3,2,1,0:T(8,128)(2,1)}, f32[8,8,32,128]{3,2,1,0:T(8,128)}, f32[8,8,32,128]{3,2,...) custom-call(bf16[8,32,2048]{2,1,0:T(8,128)(2,1)} %bitcast.39, ...), custom_call_target="tpu_custom_call" | custom-call | flops 42949672960 | bytes 167772160 | tf_op jit(solution)/shard_map/pallas_call | solution.py:283
  302.1 107.9 %shard_map.205 = (bf16[8,32,2048]{2,1,0:T(8,128)(2,1)}, f32[8,32,128]{2,1,0:T(8,128)}, bf16[8,4,2,32,2048]{4,3,2,1,0:T(8,128)(2,1)}, bf16[8,8,32,256]{3,2,1,0:T(...) custom-call(bf16[8,32,2048]{2,1,0:T(8,128)(2,1)} %get-tuple-element.37.own, ...), custom_call_target="tpu_custom_call" | custom-call | flops 27917287424 | bytes 104857600 | tf_op jit(solution)/shard_map/pallas_call | solution.py:283
  410.0 1.2 copy-done.2
  411.3 22.0 %shard_map.206 = (bf16[8,256,256]{2,1,0:T(8,128)(2,1)S(1)}, bf16[8,256,256]{2,1,0:T(8,128)(2,1)S(1)}, bf16[8,256,256]{2,1,0:T(8,128)(2,1)S(1)}) custom-call(s32[2]{0:T(128)S(1)} %get-tuple-element.65.live, s32[1,8]{1,0:T(1,128)S(1)} %copy-done, bf16[2048,768]{1,0:T(8,128)(2,1)} %bitcast.50, bf16[2048,768]{1,0:T(8,128)(2,1)} %bitcast.51, ...), custom_call_target="tpu_custom_call" | custom-call | flops 10737418240 | bytes 8388608 | tf_op jit(solution)/shard_map/pallas_call | solution.py:423
  433.3 1.0 copy-done.3
  434.3 1.0 copy-done.4
  435.2 1.0 copy-done.5
  436.2 88.3 %shard_map.207 = (f32[8,32,2048]{2,1,0:T(8,128)}, f32[3,2048]{1,0:T(4,128)}, bf16[4,3,512,256]{3,2,1,0:T(8,128)(2,1)}, bf16[4,256,512]{2,1,0:T(8,128)(2,1)}, bf16[4,512,1024]{2,1,0:T(8,128)(2,1)}) custom-call(bf16[8,256,256]{2,1,0:T(8,128)(2,1)} %copy-done.3, bf16[8,256,256]{2,1,0:T(8,128)(2,1)} %copy-done.4, ...), custom_call_target="tpu_custom_call", output_to_operand_aliasing={{4}: (9, {})} | custom-call | flops 12884901888 | bytes 62914560 | tf_op jit(solution)/shard_map/pallas_call | solution.py:283
  524.6 0.1 slice_reduce_fusion
  524.7 0.6 reshape_squeeze.3
  525.3 1.6 fusion.1
  526.9 2.2 convert_reduce_fusion.3
  529.1 3.7 convert_reduce_fusion.2
  532.8 2.3 convert_reduce_fusion.1
  535.0 0.7 copy-done.6
  535.7 2.0 convert_reduce_fusion
  537.7 1.0 copy.29
  538.7 1.3 copy.30
  (20 shorter events, 0.1 us)
Async XLA Ops:
  302.1 108.0 %copy-start = (s32[1,8]{1,0:T(1,128)S(1)}, s32[1,8]{1,0:T(1,128)}, u32[]{:S(2)}) copy-start(s32[1,8]{1,0:T(1,128)} %docs.3) | copy-start | bytes 100
  302.1 108.0 %copy-start.1 = (f32[8,8,32,128]{3,2,1,0:T(8,128)S(1)}, f32[8,8,32,128]{3,2,1,0:T(8,128)}, u32[]{:S(2)}) copy-start(f32[8,8,32,128]{3,2,1,0:T(8,128)} %get-tuple-element.46) | copy-start | bytes 3145732
  410.0 1.2 copy-start.2
  433.3 1.0 copy-start.3
  434.3 1.0 copy-start.4
  435.2 1.0 copy-start.5
  436.2 88.4 %copy-start.10 = (f32[8,32,128]{2,1,0:T(8,128)S(1)}, f32[8,32,128]{2,1,0:T(8,128)}, u32[]{:S(2)}) copy-start(f32[8,32,128]{2,1,0:T(8,128)} %get-tuple-element.58) | copy-start | bytes 393220
  525.3 7.4 %copy-start.7 = (bf16[4,512,1024]{2,1,0:T(8,128)(2,1)S(1)}, bf16[4,512,1024]{2,1,0:T(8,128)(2,1)}, u32[]{:S(2)}) copy-start(bf16[4,512,1024]{2,1,0:T(8,128)(2,1)} %get-tuple-element.62) | copy-start | bytes 12582916
  532.8 2.9 copy-start.6
  535.7 2.0 copy-start.9
  535.7 3.0 copy-start.8
where the time goes:
time: 546 us; the launch traced here: 540 us
  Pallas kernels  515 us (94%)
  local copies, waits for them, and re-layouts  13 us (2%)
  other arithmetic  10.7 us (2%)
    pallas_call x3, Pallas kernels, call(): pl.pallas_call(body, out_shape=outs, in_specs=in_specs or [VM] * len(ins)...  493 us
    pallas_call x1, Pallas kernels, attend_back(): pl.pallas_call(body, out_shape=[jax.ShapeDtypeStruct((groups, length // g...  22 us

commit v1 on v0

--- a/solution.py
+++ b/solution.py
@@ -2,6 +2,7 @@
 
 import jax
 import jax.numpy as jnp
+import numpy as np
 from jax import lax
 from jax.experimental import pallas as pl
 from jax.experimental.pallas import tpu as pltpu
@@ -19,6 +20,7 @@
 F32 = jnp.float32
 ANY = pl.BlockSpec(memory_space=pl.ANY)
 VM = pl.BlockSpec(memory_space=pltpu.VMEM)
+SM = pl.BlockSpec(memory_space=pltpu.SMEM)
 DMA = pltpu.SemaphoreType.DMA
 NT = (((1,), (1,)), ((), ()))
 TN = (((0,), (0,)), ((), ()))
@@ -366,6 +368,13 @@
     return starts_of([lengths[0, n] for n in range(lengths.shape[1])], places)[:1]
 
 
+def weight_rows(i, reach):
+    ramp = reach * (reach - 1) // 2
+    if isinstance(i, int) and i < reach:
+        return i * (i + 1) // 2 * QROWS
+    return (ramp + (i - reach + 1) * reach) * QROWS
+
+
 def put_grouped(out, block, i, own_tokens, rows, at=slice(None)):
     for n in range(0, QROWS, rows):
         rank, inside = divmod(n, own_tokens)
@@ -373,16 +382,16 @@
         out[inside // rows, pl.ds(pl.multiple_of(rank * rows, rows), rows), at] = block[n : n + rows]
 
 
-def attend_back(qkv, grad, lengths, active, cosines, sines, width, groups, own_tokens):
+def attend_back(qkv, grad, kept_weights, count, cosines, sines, width, groups, own_tokens):
     length, heads = qkv.shape[0], width // HDIM
     scaling = HDIM ** (-0.5)
     reach = MAXDOC // QROWS + 1
     rows_own = own_tokens // groups
 
-    def body(live, docs, q, k, v, g, cos, sin, g_q, g_k, g_v, k_t, sum_k, sum_v):
-        h = pl.program_id(0)
-
-        @pl.when(live[h] == 0)
+    def body(active, q, k, v, g, cos, sin, kept, g_q, g_k, g_v, k_t, sum_k, sum_v):
+        live = lax.axis_index("tensor") * heads + pl.program_id(0) < active[0]
+
+        @pl.when(jnp.logical_not(live))
         def _():
             g_q[...] = jnp.zeros_like(g_q)
             g_k[...] = jnp.zeros_like(g_k)
@@ -391,7 +400,7 @@
         def rotate_back(d, rows):
             return (d * cos[rows] + swap_halves(d * sin[rows])).astype(BF)
 
-        @pl.when(live[h] != 0)
+        @pl.when(live)
         def _():
             k_t[...] = k[...].T
             sum_k[...] = jnp.zeros_like(sum_k)
@@ -400,9 +409,9 @@
                 low = i + 1 - count
                 rows = pl.ds(pl.multiple_of(i * QROWS, QROWS), QROWS)
                 keys = pl.ds(pl.multiple_of(low * QROWS, QROWS), count * QROWS)
-                start = query_starts(docs, i * QROWS)
-                weights = softmax_block(q[rows], k[keys], start, i * QROWS, low * QROWS, scaling)
-                sum_v[keys] += dot(weights.astype(BF), g[rows])
+                weights = kept[0, pl.ds(weight_rows(i, reach), count * QROWS)]
+                sum_v[keys] += dot(weights, g[rows])
+                weights = weights.astype(F32)
                 g_weights = dot(v[keys], g[rows], NT)
                 inner = jnp.sum(weights * g_weights, axis=0, keepdims=True)
                 g_scores = (weights * (g_weights - inner)).astype(BF)
@@ -418,28 +427,33 @@
                 put_grouped(g_k, rotate_back(sum_k[rows] * scaling, rows), i, own_tokens, rows_own)
                 put_grouped(g_v, sum_v[rows].astype(BF), i, own_tokens, rows_own)
 
-    column = lambda n: pl.BlockSpec((length, HDIM), lambda h, live, docs: (0, n * heads + h))
-    table = pl.BlockSpec((length, HDIM), lambda h, live, docs: (0, 0))
+    column = lambda n: pl.BlockSpec((length, HDIM), lambda h, live: (0, n * heads + h))
+    table = pl.BlockSpec((length, HDIM), lambda h, live: (0, 0))
     return pl.pallas_call(
         body,
         out_shape=[jax.ShapeDtypeStruct((groups, length // groups, width), BF)] * 3,
         grid_spec=pltpu.PrefetchScalarGridSpec(
-            num_scalar_prefetch=2,
+            num_scalar_prefetch=1,
             grid=(heads,),
-            in_specs=[column(0), column(1), column(2), column(0), table, table],
-            out_specs=[
-                pl.BlockSpec((groups, length // groups, HDIM), lambda h, live, docs: (0, 0, h))
-            ]
-            * 3,
+            in_specs=[
+                column(0),
+                column(1),
+                column(2),
+                column(0),
+                table,
+                table,
+                pl.BlockSpec((1, *kept_weights.shape[1:]), lambda h, live: (h, 0, 0)),
+            ],
+            out_specs=[pl.BlockSpec((groups, length // groups, HDIM), lambda h, live: (0, 0, h))] * 3,
             scratch_shapes=[
                 pltpu.VMEM((HDIM, length), BF),
                 pltpu.VMEM((length, HDIM), F32),
                 pltpu.VMEM((length, HDIM), F32),
             ],
         ),
-        compiler_params=pltpu.CompilerParams(vmem_limit_bytes=48 << 20),
-        cost_estimate=pl.CostEstimate(flops=10 << 30, bytes_accessed=8 << 20, transcendentals=0),
-    )(active, lengths, qkv, qkv, qkv, grad, cosines, sines)
+        compiler_params=pltpu.CompilerParams(vmem_limit_bytes=60 << 20),
+        cost_estimate=pl.CostEstimate(flops=10 << 30, bytes_accessed=16 << 20, transcendentals=0),
+    )(count, qkv, qkv, qkv, grad, cosines, sines, kept_weights)
 
 
 class Spread:
@@ -565,7 +579,7 @@
 
 
 def front(
-    tokens, cotangent, probs, gain, lengths, frequency, live, w_qkv, w_out, g_ln, b_ln, w_up, w_down, widths, ranks
+    tokens, cotangent, probs, gain, lengths, frequency, count, w_qkv, w_out, g_ln, b_ln, w_up, w_down, widths, ranks
 ):
     width, columns = w_out.shape[0], w_up.shape[1]
     tile = min(256, columns)
@@ -587,14 +601,14 @@
     back_at = hidden_at + 2 + hops
 
     def body(
-        x_ref, dy, p, gain_ref, docs, freq, live_ref, w, wo, gain2, bias2, up, down, wide,
+        x_ref, dy, p, gain_ref, docs, freq, active, w, wo, gain2, bias2, up, down, wide,
         qkv, kept_x, cos_out, sin_out, attended, resid, kept_grad, grad_resid, grad_low, gains, kept_ln, squared,
-        hidden_grad,
+        hidden_grad, kept_weights,
         full, w_v, wo_v, dy_v, up_v, down_v, qkv_v, cos_v, sin_v, v_t, attended_v, low_v, resid_v, high_v, grad_v,
         lifted, squared_v, hidden_v,
         a_send, a_recv, a_across, b_send, b_recv, b_across, c_send, c_recv, c_across,
         part, near, far, acc, s1, s2, s3, t1, t2, t3,
-        load_sem, kept_sem, out_sem, place_sem, attended_sem, resid_sem, result_sem, tile_sem,
+        load_sem, kept_sem, out_sem, place_sem, attended_sem, resid_sem, result_sem, tile_sem, weights_v, weights_sem,
     ):
         line = Line(ranks, rows)
         loads = Loads([(w, w_v), (wo, wo_v), (dy, dy_v), (up, up_v), (down, down_v)], load_sem)
@@ -687,6 +701,14 @@
         def part_of(which, h):
             return pl.ds(pl.multiple_of((which * heads + h) * HDIM, HDIM), HDIM)
 
+        def keep_weights(i, count, h):
+            rows_kept = weight_rows(i if count == reach else count - 1, reach)
+            return pltpu.make_async_copy(
+                weights_v.at[h, pl.ds(0, count * QROWS)],
+                kept_weights.at[h, pl.ds(pl.multiple_of(rows_kept, QROWS), count * QROWS)],
+                weights_sem.at[h],
+            )
+
         def attend_block(i, count):
             low = i + 1 - count
             start = query_starts(docs, i * QROWS)
@@ -695,11 +717,18 @@
             def _(h):
                 q = qkv_v[pl.ds(i * span, span), :, :, part_of(0, h)].reshape(QROWS, HDIM)
                 k = qkv_v[pl.ds(low * span, count * span), :, :, part_of(1, h)].reshape(count * QROWS, HDIM)
-                weights = softmax_block(q, k, start, i * QROWS, low * QROWS, scaling)
+                weights = softmax_block(q, k, start, i * QROWS, low * QROWS, scaling).astype(BF)
                 keys = pl.ds(pl.multiple_of(low * QROWS, QROWS), count * QROWS)
-                done = dot(v_t[h, :, keys], weights.astype(BF)).T
-                done = (done * live_ref[:, part_of(0, h)]).astype(BF)
+                done = dot(v_t[h, :, keys], weights).T
+                done = (done * jnp.where(line.t * heads + h < active[0], 1.0, 0.0)).astype(BF)
                 put_grouped(attended_v, done, i, own_tokens, rows, part_of(0, h))
+                if not isinstance(i, int):
+                    pl.when(i == reach - 1)(lambda: keep_weights(i - 1, reach - 1, h).wait())
+                    pl.when(i > reach - 1)(lambda: keep_weights(i - 1, reach, h).wait())
+                elif i:
+                    keep_weights(i - 1, count - 1, h).wait()
+                weights_v[h, : count * QROWS] = weights
+                keep_weights(i, count, h).start()
 
         def attention(turn):
             @pl.when(turn == 0)
@@ -817,6 +846,8 @@
             within(i - back_at, groups, finish)
             within(i, lead, attention)
 
+        for h in range(heads):
+            keep_weights(blocks - 1, reach, h).wait()
         second.drain()
         third.drain()
         pl.loop(0, groups)(reduce_back.drain)
@@ -838,7 +869,7 @@
     hidden = jax.ShapeDtypeStruct((groups, tokens_all, columns), BF)
     return call(
         body,
-        [tokens, cotangent, probs, gain, lengths, frequency, live, w_qkv, w_out, g_ln, b_ln, w_up, w_down, widths],
+        [tokens, cotangent, probs, gain, lengths, frequency, count, w_qkv, w_out, g_ln, b_ln, w_up, w_down, widths],
         [
             projected,
             full,
@@ -853,6 +884,7 @@
             full,
             hidden,
             hidden,
+            jax.ShapeDtypeStruct((heads, weight_rows(blocks, reach), QROWS), BF),
         ],
         [
             *scratch_of(full, w_qkv, w_out, cotangent, w_up, w_down, projected),
@@ -874,10 +906,12 @@
             DMA,
             *[DMA((groups,))] * 3,
             DMA((4, groups)),
+            pltpu.VMEM((heads, reach * QROWS, QROWS), BF),
+            DMA((heads,)),
         ],
         0,
-        in_specs=[VM, ANY, VM, VM, pl.BlockSpec(memory_space=pltpu.SMEM), VM, VM, ANY, ANY, VM, VM, ANY, ANY, VM],
-        out_specs=[ANY] * 9 + [VM] + [ANY] * 3,
+        in_specs=[VM, ANY, VM, VM, SM, VM, SM, ANY, ANY, VM, VM, ANY, ANY, VM],
+        out_specs=[ANY] * 9 + [VM] + [ANY] * 4,
         flops=8 * length * model * (width + columns),
         moved=160 << 20,
     )
@@ -900,7 +934,7 @@
 
 
 def feed_out(
-    own_grad, squared, hidden_grad, kept_ln, branch_grad, w_down, w_out, active, resid, cotangent, probs, ranks, sequences
+    own_grad, squared, hidden_grad, kept_ln, branch_grad, w_down, w_out, count, resid, cotangent, probs, ranks, sequences
 ):
     groups, rows, model = own_grad.shape
     columns, width = w_down.shape[0], w_out.shape[0]
@@ -909,7 +943,7 @@
     half = share // 2
 
     def body(
-        own, sq, hg, ln, bg, down, w, live, res, dy, p, result, probs_grad, kept, grad, land_down, land_up,
+        own, sq, hg, ln, bg, down, w, active, res, dy, p, result, probs_grad, kept, grad, land_down, land_up,
         full, g_send, g_recv, g_across, part, near, far, acc, s1, s2, s3, kept_sem,
         out_down, down_send, down_recv, out_up, up_send, up_recv, ln_v, bg_v, fetch_sem,
         sq_v, hg_v, down_v, res_v, dy_v, load_sem, result_v, back_v, result_sem, back_sem,
@@ -926,7 +960,9 @@
         def arrived(g):
             gather.arrived(g)
             keep.put(g)
-            back = (dot(full[g].reshape(tokens, model), w[...], NT) * live[...]).astype(BF)
+            heads = line.t * (width // HDIM) + lax.broadcasted_iota(jnp.int32, (1, width), 1) // HDIM
+            live = jnp.where(heads < active[0], 1.0, 0.0)
+            back = (dot(full[g].reshape(tokens, model), w[...], NT) * live).astype(BF)
             for rank in range(ranks):
                 back_v[rank, g] = back[rank * rows : (rank + 1) * rows]
             keep_back.put(g)
@@ -945,9 +981,8 @@
             ffn = acc[...]
             result_v[g] = (res_v[g] + p[g, :, :1] * ffn).astype(BF)
             keep_result.put(g)
-            probs_grad[g] = jnp.broadcast_to(
-                jnp.sum(dy_v[g].astype(F32) * ffn, axis=1, keepdims=True), (rows, HDIM)
-            )
+            scores = jnp.sum(dy_v[g].astype(F32) * ffn, axis=1, keepdims=True)
+            probs_grad[pl.ds(g, 1)] = jnp.broadcast_to(scores, (rows, HDIM)).T[:1]
 
         def fetches(step):
             at = pl.multiple_of(to_up.target(lax.rem(step + 1, sequences)) * share, share)
@@ -1020,10 +1055,10 @@
     back = jax.ShapeDtypeStruct((ranks, groups, rows, width), BF)
     return call(
         body,
-        [own_grad, squared, hidden_grad, kept_ln, branch_grad, w_down, w_out, active, resid, cotangent, probs],
+        [own_grad, squared, hidden_grad, kept_ln, branch_grad, w_down, w_out, count, resid, cotangent, probs],
         [
             low,
-            jax.ShapeDtypeStruct((groups, rows, HDIM), F32),
+            jax.ShapeDtypeStruct((groups, rows), F32),
             kept,
             back,
             jax.ShapeDtypeStruct((sequences, columns, share), BF),
@@ -1046,7 +1081,7 @@
             DMA((groups,)),
         ],
         3,
-        in_specs=[ANY, ANY, ANY, ANY, ANY, ANY, VM, VM, ANY, ANY, VM],
+        in_specs=[ANY, ANY, ANY, ANY, ANY, ANY, VM, SM, ANY, ANY, VM],
         out_specs=[ANY, VM, ANY, ANY, ANY, ANY],
         flops=2 * groups * tokens * model * (3 * columns + width),
         moved=100 << 20,
@@ -1246,6 +1281,7 @@
 
         to_qkv.end()
         to_out.end()
+
         to_up.end()
 
     return call(
@@ -1290,6 +1326,49 @@
     )
 
 
+def collect(result, tokens_grad, totals, *landed):
+    steps = result.shape[0]
+
+    def body(result_in, tokens_in, totals_in, *refs):
+        pieces, outs = refs[: len(landed)], refs[len(landed) :]
+        outs[0][...] = result_in[...]
+        outs[1][...] = tokens_in[...]
+        for n in range(3):
+            outs[2 + n][...] = totals_in[n : n + 1]
+        for piece, out in zip(pieces, outs[5:]):
+            total = piece[0].astype(F32)
+            for n in range(1, piece.shape[0]):
+                total += piece[n].astype(F32)
+            out[...] = total
+
+    def split(a, at):
+        block = list(a.shape)
+        block[at] //= steps
+        return pl.BlockSpec(tuple(block), lambda i: tuple(i if n == at else 0 for n in range(len(block))))
+
+    sums = [jax.ShapeDtypeStruct(a.shape[1:], F32) for a in landed]
+    row = jax.ShapeDtypeStruct((1, totals.shape[1]), F32)
+    fixed = lambda a: pl.BlockSpec(a.shape, lambda i: (0, 0))
+    return pl.pallas_call(
+        body,
+        out_shape=[
+            jax.ShapeDtypeStruct(result.shape, BF),
+            jax.ShapeDtypeStruct(tokens_grad.shape, F32),
+            row,
+            row,
+            row,
+            *sums,
+        ],
+        grid=(steps,),
+        in_specs=[split(result, 0), split(tokens_grad, 0), fixed(totals)]
+        + [split(a, a.ndim - 2) for a in landed],
+        out_specs=[split(result, 0), split(tokens_grad, 0), fixed(row), fixed(row), fixed(row)]
+        + [split(a, len(a.shape) - 2) for a in sums],
+        compiler_params=pltpu.CompilerParams(vmem_limit_bytes=60 << 20),
+        cost_estimate=pl.CostEstimate(flops=1 << 24, bytes_accessed=24 << 20, transcendentals=0),
+    )(result, tokens_grad, totals, *landed)
+
+
 def shards(
     tokens,
     cotangent,
@@ -1311,37 +1390,33 @@
     sequences = lax.axis_size("dp")
     groups, rows = GROUPS, own_tokens // GROUPS
     width = w_out.shape[0]
-    heads_here = width // HDIM
     half = HDIM // 2
-    frequency = 10000.0 ** (-jnp.arange(half, dtype=F32) / half)
-    frequency = jnp.concatenate([frequency, frequency]).reshape(1, HDIM)
+    frequency = 10000.0 ** (-np.arange(half) / half)
+    frequency = jnp.asarray(np.concatenate([frequency, frequency]).reshape(1, HDIM), F32)
     w_qkv_t = w_qkv.transpose(1, 0, 2)
     x = tokens.reshape(groups, rows, model)
     dy = cotangent.reshape(groups, rows, model)
     first_norm_gain, g_ln, b_ln = (v.reshape(1, model) for v in (first_norm_gain, g_ln, b_ln))
     p = jnp.broadcast_to(probs.reshape(groups, rows, 1), (groups, rows, HDIM))
-    head_ids = lax.axis_index("tensor") * heads_here + jnp.arange(heads_here, dtype=jnp.int32)
-    active = (head_ids < head_count[0]).astype(jnp.int32)
-    live = jnp.repeat(active.astype(F32), HDIM).reshape(1, width)
     wide = widths.reshape(ranks, groups, rows).swapaxes(0, 1).reshape(groups, ranks * rows)
 
     (
         qkv, kept_x, cosines, sines, attended, resid, kept_ffn_grad, grad_resid, grad_low, gains, kept_ln, squared,
-        grad_hidden,
+        grad_hidden, kept_weights,
     ) = front(
-        x, dy, p, first_norm_gain, lengths, frequency, live, w_qkv_t, w_out, g_ln, b_ln, w_up, w_down, wide, ranks
+        x, dy, p, first_norm_gain, lengths, frequency, head_count, w_qkv_t, w_out, g_ln, b_ln, w_up, w_down, wide, ranks
     )
     qkv = qkv.reshape(length_all, 3 * width)
     cosines, sines = cosines.reshape(length_all, HDIM), sines.reshape(length_all, HDIM)
     whole = lambda kept: kept.reshape(groups, ranks * rows, model)
     result, probs_grad, kept_attn_grad, grad_attended, land_down, land_up = feed_out(
-        grad_low, squared, grad_hidden, whole(kept_ln), whole(kept_ffn_grad), w_down, w_out, live, resid, dy, p, ranks, sequences
+        grad_low, squared, grad_hidden, whole(kept_ln), whole(kept_ffn_grad), w_down, w_out, head_count, resid, dy, p, ranks, sequences
     )
     grad_proj = attend_back(
         qkv,
         grad_attended.reshape(length_all, width),
-        lengths,
-        active,
+        kept_weights,
+        head_count,
         cosines,
         sines,
         width,
@@ -1352,18 +1427,20 @@
         grad_proj, w_qkv_t, whole(kept_x), attended, whole(kept_attn_grad), whole(kept_ln), grad_hidden, land_up, x, first_norm_gain,
         grad_resid, gains, ranks, sequences,
     )
-    add_up = lambda landed: jnp.sum(landed.astype(F32), axis=0)
+    result, tokens_grad, rms, gain, bias, g_qkv, g_out, g_up, g_down = collect(
+        result, tokens_grad, totals, land_qkv, land_out, land_up, land_down
+    )
     return (
         result.reshape(own_tokens, model),
         tokens_grad.reshape(own_tokens, model),
-        probs_grad[:, :, 0].reshape(own_tokens),
-        totals[0],
-        add_up(land_qkv).transpose(1, 0, 2),
-        add_up(land_out),
-        totals[1],
-        totals[2],
-        add_up(land_up),
-        add_up(land_down),
+        probs_grad.reshape(own_tokens),
+        rms.reshape(model),
+        g_qkv.transpose(1, 0, 2),
+        g_out,
+        gain.reshape(model),
+        bias.reshape(model),
+        g_up,
+        g_down,
     )
 
 

time: 546 us -> 533 us (0.976)
  other arithmetic: 10.7 us -> 0 us
  local copies, waits for them, and re-layouts: 13 us -> 3.61 us
  Pallas kernels: 515 us -> 522 us
    pallas_call x0 -> x1, Pallas kernels: none -> 10.9 us  [collect(): pl.pallas_call(body, out_shape=[jax.ShapeDtypeStruct(result.shape, BF), j...]
    reduce_sum x4 -> x0, other arithmetic: 10.1 us -> none  [shards(): add_up = lambda landed: jnp.sum(landed.astype(F32), axis=0)]
    unnamed x24 -> x2, local copies, waits for them, and re-layouts: 7.09 us -> 0.01 us
where the time goes in v1:
time: 533 us; the launch traced here: 526 us
  Pallas kernels  522 us (98%)
    pallas_call x3, Pallas kernels, call(): pl.pallas_call(body, out_shape=outs, in_specs=in_specs or [VM] * len(ins)...  493 us
    pallas_call x1, Pallas kernels, attend_back(): pl.pallas_call(body, out_shape=[jax.ShapeDtypeStruct((groups, length // g...  17.6 us
    pallas_call x1, Pallas kernels, collect(): pl.pallas_call(body, out_shape=[jax.ShapeDtypeStruct(result.shape, BF), j...  10.9 us

profile of v1, /device:TPU:0, one launch (start us, length us, event | category | flops | bytes accessed | tf_op | source)
XLA Modules:
  0.0 526.5 jit_solution(13963177774591056313)
XLA Ops:
  1.3 0.8 broadcast_in_dim.7
  2.0 0.8 reshape.91
  2.8 0.7 reshape.92.wide
  3.5 0.8 broadcast_in_dim.8.p
  4.3 297.1 %shard_map.213 = (bf16[8,8,32,768]{3,2,1,0:T(8,128)(2,1)}, bf16[8,4,2,32,2048]{4,3,2,1,0:T(8,128)(2,1)}, f32[8,8,32,128]{3,2,1,0:T(8,128)}, f32[8,8,32,128]{3,2,...) custom-call(bf16[8,32,2048]{2,1,0:T(8,128)(2,1)} %bitcast.28, ...), custom_call_target="tpu_custom_call" | custom-call | flops 42949672960 | bytes 167772160 | tf_op jit(solution)/shard_map/pallas_call | solution.py:285
  301.3 107.7 %shard_map.214 = (bf16[8,32,2048]{2,1,0:T(8,128)(2,1)}, f32[8,32]{1,0:T(8,128)}, bf16[8,4,2,32,2048]{4,3,2,1,0:T(8,128)(2,1)}, bf16[8,8,32,256]{3,2,1,0:T(8,128)...) custom-call(bf16[8,32,2048]{2,1,0:T(8,128)(2,1)} %get-tuple-element.47.own, ...), custom_call_target="tpu_custom_call" | custom-call | flops 27917287424 | bytes 104857600 | tf_op jit(solution)/shard_map/pallas_call | solution.py:285
  409.0 17.6 %shard_map.215 = (bf16[8,256,256]{2,1,0:T(8,128)(2,1)}, bf16[8,256,256]{2,1,0:T(8,128)(2,1)}, bf16[8,256,256]{2,1,0:T(8,128)(2,1)}) custom-call(s32[1]{0:T(128)S(6)} %copy.27.active, bf16[2048,768]{1,0:T(8,128)(2,1)} %bitcast.43, bf16[2048,768]{1,0:T(8,128)(2,1)} %bitcast.44, bf16[2048,768]{1,0:T(8,128)(2,1)} %bitcast.45, bf16[2048,256]{1,0:T(8,128)(2,1)} %bitcast.48, ...), custom_call_target="tpu_custom_call" | custom-call | flops 10737418240 | bytes 16777216 | tf_op jit(solution)/shard_map/pallas_call | solution.py:432
  426.6 88.3 %shard_map.216 = (f32[8,32,2048]{2,1,0:T(8,128)}, f32[3,2048]{1,0:T(4,128)}, bf16[4,3,512,256]{3,2,1,0:T(8,128)(2,1)}, bf16[4,256,512]{2,1,0:T(8,128)(2,1)}, bf16[4,512,1024]{2,1,0:T(8,128)(2,1)}) custom-call(bf16[8,256,256]{2,1,0:T(8,128)(2,1)} %get-tuple-element.59.gq, bf16[8,256,256]{2,1,0:T(8,128)(2,1)} %get-tuple-element.60.gk, ...), custom_call_target="tpu_custom_call", output_to_operand_aliasing={{4}: (9, {})} | custom-call | flops 12884901888 | bytes 62914560 | tf_op jit(solution)/shard_map/pallas_call | solution.py:285
  514.9 0.0 copy-start
  514.9 10.9 %shard_map.217 = (bf16[8,32,2048]{2,1,0:T(8,128)(2,1)}, f32[8,32,2048]{2,1,0:T(8,128)}, f32[1,2048]{1,0:T(1,128)}, f32[1,2048]{1,0:T(1,128)}, f32[1,2048]{1,0:T(...) custom-call(bf16[8,32,2048]{2,1,0:T(8,128)(2,1)} %get-tuple-element.53.result_i, ...), custom_call_target="tpu_custom_call" | custom-call | flops 16777216 | bytes 25165824 | tf_op jit(solution)/shard_map/pallas_call | solution.py:1352
  525.8 0.0 copy-done
  525.9 0.6 reshape.103
  (1 shorter events, 0.0 us)
Async XLA Ops:
  514.9 10.9 %copy-start = (f32[8,32]{1,0:T(8,128)S(1)}, f32[8,32]{1,0:T(8,128)}, u32[]{:S(2)}) copy-start(f32[8,32]{1,0:T(8,128)} %get-tuple-element.76) | copy-start | bytes 3076

commit v2 on v1

--- a/solution.py
+++ b/solution.py
@@ -300,7 +300,7 @@
     hops = line.chips - 1
     produce = list(produce)
     between = len(produce) > 1
-    turns = groups + hops + 1 + (lead + 1 if reduce else 0)
+    turns = groups + hops + 1 + (lead if reduce else 0)
 
     @pl.loop(0, turns)
     def _(i):
@@ -330,7 +330,7 @@
                 reduce.last(g)
                 finish(g)
 
-            within(i - lead - 2 - hops, groups, end)
+            within(i - lead - 1 - hops, groups, end)
         if extra:
             within(i, min(extra[0], turns), extra[1])
 
@@ -593,12 +593,12 @@
     reach = MAXDOC // QROWS + 1
     span = QROWS // own_tokens
     blocks = length // QROWS
-    lead = 2
+    lead, ahead = 2, 3
     hops = chips - 1
     tokens_all = ranks * rows
-    normed_at = lead + 2 + hops
+    normed_at = lead + 1 + hops
     hidden_at = normed_at + hops + 1
-    back_at = hidden_at + 2 + hops
+    back_at = hidden_at + 1 + hops
 
     def body(
         x_ref, dy, p, gain_ref, docs, freq, active, w, wo, gain2, bias2, up, down, wide,
@@ -628,6 +628,13 @@
         ]
         place_grad = pltpu.make_async_copy(low_v, kept_grad.at[:, line.z, line.c], place_sem)
 
+        second = Gather(line, kept_grad, b_send, b_recv, b_across)
+
+        def second_turn(j):
+            for h in range(hops, 0, -1):
+                within(j - h, groups, functools.partial(second.hop, h=h))
+            within(j, groups, second.begin)
+
         def scale_grad(turn):
             loads.begin(turn == 0, 0, 1, 2)
 
@@ -640,6 +647,9 @@
                     low_v[g] = (dy_v[g].astype(F32) * p[g, :, :1]).astype(BF)
 
                 place_grad.start()
+
+            pl.when(turn == 2)(place_grad.wait)
+            second_turn(turn - groups - hops - 1 + ahead)
 
         def project(g):
             r = lax.broadcasted_iota(jnp.int32, (ranks * rows, HDIM), 0)
@@ -671,7 +681,7 @@
             for store in stores:
                 store.put(g)
 
-        stream(line, groups, gather, arrived=project, extra=(2, scale_grad))
+        stream(line, groups, gather, arrived=project, extra=(groups + hops + 1, scale_grad))
 
         @pl.loop(0, groups)
         def _(g):
@@ -680,7 +690,6 @@
 
         tables.end(groups)
         loads.begin(True, 3, 4)
-        second = Gather(line, kept_grad, b_send, b_recv, b_across)
         third = Gather(line, full, c_send, c_recv, c_across)
         reduce = Reduce(line, part, near, far, acc, s1, s2, s3)
         reduce_back = Reduce(line, part, near, far, acc, t1, t2, t3)
@@ -692,7 +701,6 @@
         hiddens = Turns([(squared_v, squared), (hidden_v, hidden_grad)], tile_sem.at[pl.ds(2, 2)])
         gains[...] = jnp.zeros_like(gains)
         first_column = line.t * columns
-        place_grad.wait()
 
         def fetch(g):
             slot = lax.rem(g, 2)
@@ -832,17 +840,17 @@
                 within(i - hidden_at - 1 - hops + d, groups, functools.partial(reduce_back.step, d=d))
                 within(i - normed_at - h, groups, functools.partial(third.hop, h=h))
                 within(i - lead - 1 - hops + d, groups, functools.partial(reduce.step, d=d))
-                within(i - h, groups, functools.partial(second.hop, h=h))
+                within(i + ahead - h, groups, functools.partial(second.hop, h=h))
                 if n == 0:
                     within(i - hidden_at, groups, arrived)
                 for piece in (forward, backward, lower)[n * 3 // hops : (n + 1) * 3 // hops]:
                     within(i - hidden_at, groups, piece)
-            within(i, groups, second.begin)
+            within(i + ahead, groups, second.begin)
             within(i - hidden_at, groups, reduce_back.begin)
             within(i - normed_at, groups, norm)
             within(i - lead, groups, produce)
             within(i - lead, groups, reduce.begin)
-            within(i - hops - 1, groups, second.arrived)
+            within(i + ahead - hops - 1, groups, second.arrived)
             within(i - back_at, groups, finish)
             within(i, lead, attention)
 

time: 533 us -> 528 us (level)
  Pallas kernels: 522 us -> 516 us
    pallas_call x3, Pallas kernels: 493 us -> 487 us  [call(): pl.pallas_call(body, out_shape=outs, in_specs=in_specs or [VM] * len(ins)...]
where the time goes in v2:
time: 528 us; the launch traced here: 521 us
  Pallas kernels  516 us (98%)
    pallas_call x3, Pallas kernels, call(): pl.pallas_call(body, out_shape=outs, in_specs=in_specs or [VM] * len(ins)...  487 us
    pallas_call x1, Pallas kernels, attend_back(): pl.pallas_call(body, out_shape=[jax.ShapeDtypeStruct((groups, length // g...  17.6 us
    pallas_call x1, Pallas kernels, collect(): pl.pallas_call(body, out_shape=[jax.ShapeDtypeStruct(result.shape, BF), j...  10.9 us

profile of v2, /device:TPU:0, one launch (start us, length us, event | category | flops | bytes accessed | tf_op | source)
XLA Modules:
  0.0 520.8 jit_solution(14244595500487279408)
XLA Ops:
  1.3 0.8 broadcast_in_dim.7
  2.0 0.8 reshape.91
  2.8 0.7 reshape.92.wide
  3.5 0.8 broadcast_in_dim.8.p
  4.3 292.9 %shard_map.213 = (bf16[8,8,32,768]{3,2,1,0:T(8,128)(2,1)}, bf16[8,4,2,32,2048]{4,3,2,1,0:T(8,128)(2,1)}, f32[8,8,32,128]{3,2,1,0:T(8,128)}, f32[8,8,32,128]{3,2,...) custom-call(bf16[8,32,2048]{2,1,0:T(8,128)(2,1)} %bitcast.28, ...), custom_call_target="tpu_custom_call" | custom-call | flops 42949672960 | bytes 167772160 | tf_op jit(solution)/shard_map/pallas_call | solution.py:285
  297.2 106.1 %shard_map.214 = (bf16[8,32,2048]{2,1,0:T(8,128)(2,1)}, f32[8,32]{1,0:T(8,128)}, bf16[8,4,2,32,2048]{4,3,2,1,0:T(8,128)(2,1)}, bf16[8,8,32,256]{3,2,1,0:T(8,128)...) custom-call(bf16[8,32,2048]{2,1,0:T(8,128)(2,1)} %get-tuple-element.47.own, ...), custom_call_target="tpu_custom_call" | custom-call | flops 27917287424 | bytes 104857600 | tf_op jit(solution)/shard_map/pallas_call | solution.py:285
  403.3 17.6 %shard_map.215 = (bf16[8,256,256]{2,1,0:T(8,128)(2,1)}, bf16[8,256,256]{2,1,0:T(8,128)(2,1)}, bf16[8,256,256]{2,1,0:T(8,128)(2,1)}) custom-call(s32[1]{0:T(128)S(6)} %copy.27.active, bf16[2048,768]{1,0:T(8,128)(2,1)} %bitcast.43, bf16[2048,768]{1,0:T(8,128)(2,1)} %bitcast.44, bf16[2048,768]{1,0:T(8,128)(2,1)} %bitcast.45, bf16[2048,256]{1,0:T(8,128)(2,1)} %bitcast.48, ...), custom_call_target="tpu_custom_call" | custom-call | flops 10737418240 | bytes 16777216 | tf_op jit(solution)/shard_map/pallas_call | solution.py:432
  420.9 88.3 %shard_map.216 = (f32[8,32,2048]{2,1,0:T(8,128)}, f32[3,2048]{1,0:T(4,128)}, bf16[4,3,512,256]{3,2,1,0:T(8,128)(2,1)}, bf16[4,256,512]{2,1,0:T(8,128)(2,1)}, bf16[4,512,1024]{2,1,0:T(8,128)(2,1)}) custom-call(bf16[8,256,256]{2,1,0:T(8,128)(2,1)} %get-tuple-element.59.gq, bf16[8,256,256]{2,1,0:T(8,128)(2,1)} %get-tuple-element.60.gk, ...), custom_call_target="tpu_custom_call", output_to_operand_aliasing={{4}: (9, {})} | custom-call | flops 12884901888 | bytes 62914560 | tf_op jit(solution)/shard_map/pallas_call | solution.py:285
  509.2 0.0 copy-start
  509.2 10.9 %shard_map.217 = (bf16[8,32,2048]{2,1,0:T(8,128)(2,1)}, f32[8,32,2048]{2,1,0:T(8,128)}, f32[1,2048]{1,0:T(1,128)}, f32[1,2048]{1,0:T(1,128)}, f32[1,2048]{1,0:T(...) custom-call(bf16[8,32,2048]{2,1,0:T(8,128)(2,1)} %get-tuple-element.53.result_i, ...), custom_call_target="tpu_custom_call" | custom-call | flops 16777216 | bytes 25165824 | tf_op jit(solution)/shard_map/pallas_call | solution.py:1360
  520.1 0.0 copy-done
  520.1 0.6 reshape.103
  (1 shorter events, 0.0 us)
Async XLA Ops:
  509.2 10.9 %copy-start = (f32[8,32]{1,0:T(8,128)S(1)}, f32[8,32]{1,0:T(8,128)}, u32[]{:S(2)}) copy-start(f32[8,32]{1,0:T(8,128)} %get-tuple-element.76) | copy-start | bytes 3076

commit v3 on v2

--- a/solution.py
+++ b/solution.py
@@ -40,7 +40,7 @@
         self.down = jnp.maximum(self.t - 2, 0)
         self.partner = self.t + 1 - 2 * self.c
 
-    def barrier(self, dp_size=0):
+    def greet(self, dp_size=0):
         sem = pltpu.get_barrier_semaphore()
         pl.semaphore_signal(sem, inc=1, device_id={"tensor": self.partner}, device_id_type=MESH)
 
@@ -57,10 +57,12 @@
             pl.semaphore_signal(
                 sem, inc=1, device_id={"dp": lax.rem(d + step, dp_size)}, device_id_type=MESH
             )
+
+    def meet(self, dp_size=0):
         links = self.has_up.astype(jnp.int32) + self.has_down.astype(jnp.int32)
-        pl.semaphore_wait(sem, 1 + max(dp_size - 1, 0) + links)
-
-    def barrier_all(self, dp_size):
+        pl.semaphore_wait(pltpu.get_barrier_semaphore(), 1 + max(dp_size - 1, 0) + links)
+
+    def greet_all(self, dp_size):
         sem = pltpu.get_barrier_semaphore()
         for n in range(1, self.ranks):
             pl.semaphore_signal(
@@ -71,7 +73,9 @@
             pl.semaphore_signal(
                 sem, inc=1, device_id={"dp": lax.rem(d + n, dp_size)}, device_id_type=MESH
             )
-        pl.semaphore_wait(sem, self.ranks - 1 + dp_size - 1)
+
+    def meet_all(self, dp_size):
+        pl.semaphore_wait(pltpu.get_barrier_semaphore(), self.ranks - 1 + dp_size - 1)
 
 
 def copy_to(src, dst, send, recv, rank):
@@ -611,16 +615,21 @@
         load_sem, kept_sem, out_sem, place_sem, attended_sem, resid_sem, result_sem, tile_sem, weights_v, weights_sem,
     ):
         line = Line(ranks, rows)
+        line.greet()
         loads = Loads([(w, w_v), (wo, wo_v), (dy, dy_v), (up, up_v), (down, down_v)], load_sem)
 
-        @pl.loop(0, groups)
-        def _(g):
-            x = x_ref[g].astype(F32)
-            normal = x * lax.rsqrt(row_mean(x * x) + EPSILON) * gain_ref[...]
-            full[g, line.z, line.c] = normal.astype(BF)
-
-        line.barrier()
         gather = Gather(line, full, a_send, a_recv, a_across)
+
+        class NormedFirst:
+            hop, drain = gather.hop, gather.drain
+
+            def begin(g):
+                x = x_ref[g].astype(F32)
+                normal = x * lax.rsqrt(row_mean(x * x) + EPSILON) * gain_ref[...]
+                full[g, line.z, line.c] = normal.astype(BF)
+                gather.begin(g)
+
+        line.meet()
         tables = Turns([(cos_v, cos_out), (sin_v, sin_out)], out_sem.at[pl.ds(1, 2)], lambda ref, g: ref.at[:, g])
         stores = [
             Store(full, kept_x, kept_sem.at[0]),
@@ -681,7 +690,7 @@
             for store in stores:
                 store.put(g)
 
-        stream(line, groups, gather, arrived=project, extra=(groups + hops + 1, scale_grad))
+        stream(line, groups, NormedFirst, arrived=project, extra=(groups + hops + 1, scale_grad))
 
         @pl.loop(0, groups)
         def _(g):
@@ -957,6 +966,7 @@
         sq_v, hg_v, down_v, res_v, dy_v, load_sem, result_v, back_v, result_sem, back_sem,
     ):
         line = Line(ranks, rows)
+        line.greet(sequences)
         gather = Gather(line, full, g_send, g_recv, g_across)
         reduce = Reduce(line, part, near, far, acc, s1, s2, s3)
         to_down = Spread(sequences, out_down, land_down, down_send, down_recv)
@@ -1044,7 +1054,7 @@
             load_sem,
         )
         loads.begin(True, 5)
-        line.barrier(sequences)
+        line.meet(sequences)
         loads.need(True, 5)
         stream(
             line, groups, gather, arrived, reduce, [produce], finish, 1, (max(sequences + 1, 4), beside)
@@ -1115,6 +1125,7 @@
         mine, terms, t_send, t_recv, sums, d_send, d_recv, g_q, g_k, g_v, grad_v, grad_sem,
     ):
         line = Line(ranks, rows)
+        line.greet_all(sequences)
         me = lax.axis_index("dp")
         reduce = Reduce(line, part, near, far, acc, s1, s2, s3)
         to_qkv = Spread(sequences, out_qkv, land_qkv, qkv_send, qkv_recv)
@@ -1278,9 +1289,14 @@
                     total += sums[n]
                 totals[...] = total
 
-        line.barrier_all(sequences)
+        produce(0)
+        line.meet_all(sequences)
+
+        def next_part(g):
+            pl.when(g > 0)(lambda: produce(g))
+
         stream(
-            line, groups, None, None, reduce, [produce], finish, extra=(max(groups + 3, 2 * sequences + 1), beside)
+            line, groups, None, None, reduce, [next_part], finish, extra=(max(groups + 3, 2 * sequences + 1), beside)
         )
 
         @pl.loop(0, groups)
@@ -1335,7 +1351,7 @@
 
 
 def collect(result, tokens_grad, totals, *landed):
-    steps = result.shape[0]
+    steps = result.shape[0] // 2
 
     def body(result_in, tokens_in, totals_in, *refs):
         pieces, outs = refs[: len(landed)], refs[len(landed) :]

time: 528 us -> 525 us (level)
  no operation moved by 1% of the time
where the time goes in v3:
time: 525 us; the launch traced here: 518 us
  Pallas kernels  513 us (98%)
    pallas_call x3, Pallas kernels, call(): pl.pallas_call(body, out_shape=outs, in_specs=in_specs or [VM] * len(ins)...  487 us
    pallas_call x1, Pallas kernels, attend_back(): pl.pallas_call(body, out_shape=[jax.ShapeDtypeStruct((groups, length // g...  17.6 us

profile of v3, /device:TPU:0, one launch (start us, length us, event | category | flops | bytes accessed | tf_op | source)
XLA Modules:
  0.0 518.4 jit_solution(11547974932059660805)
XLA Ops:
  1.3 0.8 broadcast_in_dim.7
  2.0 0.8 reshape.91
  2.8 0.7 reshape.92.wide
  3.5 0.8 broadcast_in_dim.8.p
  4.3 292.0 %shard_map.213 = (bf16[8,8,32,768]{3,2,1,0:T(8,128)(2,1)}, bf16[8,4,2,32,2048]{4,3,2,1,0:T(8,128)(2,1)}, f32[8,8,32,128]{3,2,1,0:T(8,128)}, f32[8,8,32,128]{3,2,...) custom-call(bf16[8,32,2048]{2,1,0:T(8,128)(2,1)} %bitcast.28, ...), custom_call_target="tpu_custom_call" | custom-call | flops 42949672960 | bytes 167772160 | tf_op jit(solution)/shard_map/pallas_call | solution.py:289
  296.3 106.1 %shard_map.214 = (bf16[8,32,2048]{2,1,0:T(8,128)(2,1)}, f32[8,32]{1,0:T(8,128)}, bf16[8,4,2,32,2048]{4,3,2,1,0:T(8,128)(2,1)}, bf16[8,8,32,256]{3,2,1,0:T(8,128)...) custom-call(bf16[8,32,2048]{2,1,0:T(8,128)(2,1)} %get-tuple-element.47.own, ...), custom_call_target="tpu_custom_call" | custom-call | flops 27917287424 | bytes 104857600 | tf_op jit(solution)/shard_map/pallas_call | solution.py:289
  402.4 17.6 %shard_map.215 = (bf16[8,256,256]{2,1,0:T(8,128)(2,1)}, bf16[8,256,256]{2,1,0:T(8,128)(2,1)}, bf16[8,256,256]{2,1,0:T(8,128)(2,1)}) custom-call(s32[1]{0:T(128)S(6)} %copy.27.active, bf16[2048,768]{1,0:T(8,128)(2,1)} %bitcast.43, bf16[2048,768]{1,0:T(8,128)(2,1)} %bitcast.44, bf16[2048,768]{1,0:T(8,128)(2,1)} %bitcast.45, bf16[2048,256]{1,0:T(8,128)(2,1)} %bitcast.48, ...), custom_call_target="tpu_custom_call" | custom-call | flops 10737418240 | bytes 16777216 | tf_op jit(solution)/shard_map/pallas_call | solution.py:436
  419.9 88.6 %shard_map.216 = (f32[8,32,2048]{2,1,0:T(8,128)}, f32[3,2048]{1,0:T(4,128)}, bf16[4,3,512,256]{3,2,1,0:T(8,128)(2,1)}, bf16[4,256,512]{2,1,0:T(8,128)(2,1)}, bf16[4,512,1024]{2,1,0:T(8,128)(2,1)}) custom-call(bf16[8,256,256]{2,1,0:T(8,128)(2,1)} %get-tuple-element.59.gq, bf16[8,256,256]{2,1,0:T(8,128)(2,1)} %get-tuple-element.60.gk, ...), custom_call_target="tpu_custom_call", output_to_operand_aliasing={{4}: (9, {})} | custom-call | flops 12884901888 | bytes 62914560 | tf_op jit(solution)/shard_map/pallas_call | solution.py:289
  508.5 0.0 copy-start
  508.5 9.2 %shard_map.217 = (bf16[8,32,2048]{2,1,0:T(8,128)(2,1)}, f32[8,32,2048]{2,1,0:T(8,128)}, f32[1,2048]{1,0:T(1,128)}, f32[1,2048]{1,0:T(1,128)}, f32[1,2048]{1,0:T(...) custom-call(bf16[8,32,2048]{2,1,0:T(8,128)(2,1)} %get-tuple-element.53.result_i, ...), custom_call_target="tpu_custom_call" | custom-call | flops 16777216 | bytes 25165824 | tf_op jit(solution)/shard_map/pallas_call | solution.py:1376
  517.7 0.0 copy-done
  517.8 0.6 reshape.103
  (1 shorter events, 0.0 us)
Async XLA Ops:
  508.5 9.2 %copy-start = (f32[8,32]{1,0:T(8,128)S(1)}, f32[8,32]{1,0:T(8,128)}, u32[]{:S(2)}) copy-start(f32[8,32]{1,0:T(8,128)} %get-tuple-element.76) | copy-start | bytes 3076

commit v4 on v3

--- a/solution.py
+++ b/solution.py
@@ -572,6 +572,10 @@
     return [pltpu.VMEM(a.shape, a.dtype) for a in arrays]
 
 
+def column_of(ref, g):
+    return jnp.broadcast_to(ref[pl.ds(g, 1), :], (HDIM, ref.shape[1])).T[:, :1]
+
+
 def row_mean(field):
     return jnp.mean(field, axis=1, keepdims=True)
 
@@ -653,7 +657,7 @@
 
                 @pl.loop(0, groups)
                 def _(g):
-                    low_v[g] = (dy_v[g].astype(F32) * p[g, :, :1]).astype(BF)
+                    low_v[g] = (dy_v[g].astype(F32) * column_of(p, g)).astype(BF)
 
                 place_grad.start()
 
@@ -847,8 +851,8 @@
             for n in range(hops):
                 h, d = hops - n, n + 1
                 within(i - hidden_at - 1 - hops + d, groups, functools.partial(reduce_back.step, d=d))
+                within(i - lead - 1 - hops + d, groups, functools.partial(reduce.step, d=d))
                 within(i - normed_at - h, groups, functools.partial(third.hop, h=h))
-                within(i - lead - 1 - hops + d, groups, functools.partial(reduce.step, d=d))
                 within(i + ahead - h, groups, functools.partial(second.hop, h=h))
                 if n == 0:
                     within(i - hidden_at, groups, arrived)
@@ -997,7 +1001,7 @@
         def finish(g):
             loads.need(g == 0, 3, 4)
             ffn = acc[...]
-            result_v[g] = (res_v[g] + p[g, :, :1] * ffn).astype(BF)
+            result_v[g] = (res_v[g] + column_of(p, g) * ffn).astype(BF)
             keep_result.put(g)
             scores = jnp.sum(dy_v[g].astype(F32) * ffn, axis=1, keepdims=True)
             probs_grad[pl.ds(g, 1)] = jnp.broadcast_to(scores, (rows, HDIM)).T[:1]
@@ -1421,7 +1425,7 @@
     x = tokens.reshape(groups, rows, model)
     dy = cotangent.reshape(groups, rows, model)
     first_norm_gain, g_ln, b_ln = (v.reshape(1, model) for v in (first_norm_gain, g_ln, b_ln))
-    p = jnp.broadcast_to(probs.reshape(groups, rows, 1), (groups, rows, HDIM))
+    p = probs.reshape(groups, rows)
     wide = widths.reshape(ranks, groups, rows).swapaxes(0, 1).reshape(groups, ranks * rows)
 
     (

time: 525 us -> 526 us (level)
  no operation moved by 1% of the time
where the time goes in v4:
time: 526 us; the launch traced here: 520 us
  Pallas kernels  515 us (98%)
    pallas_call x3, Pallas kernels, call(): pl.pallas_call(body, out_shape=outs, in_specs=in_specs or [VM] * len(ins)...  488 us
    pallas_call x1, Pallas kernels, attend_back(): pl.pallas_call(body, out_shape=[jax.ShapeDtypeStruct((groups, length // g...  17.6 us

profile of v4, /device:TPU:0, one launch (start us, length us, event | category | flops | bytes accessed | tf_op | source)
XLA Modules:
  0.0 519.9 jit_solution(7055063330591072100)
XLA Ops:
  1.3 1.3 reshape.89.p
  2.6 0.8 reshape.93
  3.4 0.7 reshape.94.wide
  4.1 292.1 %shard_map.213 = (bf16[8,8,32,768]{3,2,1,0:T(8,128)(2,1)}, bf16[8,4,2,32,2048]{4,3,2,1,0:T(8,128)(2,1)}, f32[8,8,32,128]{3,2,1,0:T(8,128)}, f32[8,8,32,128]{3,2,...) custom-call(bf16[8,32,2048]{2,1,0:T(8,128)(2,1)} %bitcast.28, ...), custom_call_target="tpu_custom_call" | custom-call | flops 42949672960 | bytes 167772160 | tf_op jit(solution)/shard_map/pallas_call | solution.py:289
  296.2 107.7 %shard_map.214 = (bf16[8,32,2048]{2,1,0:T(8,128)(2,1)}, f32[8,32]{1,0:T(8,128)}, bf16[8,4,2,32,2048]{4,3,2,1,0:T(8,128)(2,1)}, bf16[8,8,32,256]{3,2,1,0:T(8,128)...) custom-call(bf16[8,32,2048]{2,1,0:T(8,128)(2,1)} %get-tuple-element.47.own, ...), custom_call_target="tpu_custom_call" | custom-call | flops 27917287424 | bytes 104857600 | tf_op jit(solution)/shard_map/pallas_call | solution.py:289
  403.9 17.6 %shard_map.215 = (bf16[8,256,256]{2,1,0:T(8,128)(2,1)}, bf16[8,256,256]{2,1,0:T(8,128)(2,1)}, bf16[8,256,256]{2,1,0:T(8,128)(2,1)}) custom-call(s32[1]{0:T(128)S(6)} %copy.27.active, bf16[2048,768]{1,0:T(8,128)(2,1)} %bitcast.43, bf16[2048,768]{1,0:T(8,128)(2,1)} %bitcast.44, bf16[2048,768]{1,0:T(8,128)(2,1)} %bitcast.45, bf16[2048,256]{1,0:T(8,128)(2,1)} %bitcast.48, ...), custom_call_target="tpu_custom_call" | custom-call | flops 10737418240 | bytes 16777216 | tf_op jit(solution)/shard_map/pallas_call | solution.py:436
  421.5 88.6 %shard_map.216 = (f32[8,32,2048]{2,1,0:T(8,128)}, f32[3,2048]{1,0:T(4,128)}, bf16[4,3,512,256]{3,2,1,0:T(8,128)(2,1)}, bf16[4,256,512]{2,1,0:T(8,128)(2,1)}, bf16[4,512,1024]{2,1,0:T(8,128)(2,1)}) custom-call(bf16[8,256,256]{2,1,0:T(8,128)(2,1)} %get-tuple-element.59.gq, bf16[8,256,256]{2,1,0:T(8,128)(2,1)} %get-tuple-element.60.gk, ...), custom_call_target="tpu_custom_call", output_to_operand_aliasing={{4}: (9, {})} | custom-call | flops 12884901888 | bytes 62914560 | tf_op jit(solution)/shard_map/pallas_call | solution.py:289
  510.0 0.0 copy-start
  510.0 9.2 %shard_map.217 = (bf16[8,32,2048]{2,1,0:T(8,128)(2,1)}, f32[8,32,2048]{2,1,0:T(8,128)}, f32[1,2048]{1,0:T(1,128)}, f32[1,2048]{1,0:T(1,128)}, f32[1,2048]{1,0:T(...) custom-call(bf16[8,32,2048]{2,1,0:T(8,128)(2,1)} %get-tuple-element.53.result_i, ...), custom_call_target="tpu_custom_call" | custom-call | flops 16777216 | bytes 25165824 | tf_op jit(solution)/shard_map/pallas_call | solution.py:1380
  519.3 0.0 copy-done
  519.3 0.6 reshape.105
  (1 shorter events, 0.0 us)
Async XLA Ops:
  510.0 9.2 %copy-start = (f32[8,32]{1,0:T(8,128)S(1)}, f32[8,32]{1,0:T(8,128)}, u32[]{:S(2)}) copy-start(f32[8,32]{1,0:T(8,128)} %get-tuple-element.76) | copy-start | bytes 3076
